TPU v7x, 128 devices: a whole 4x4x4 slice. The times are simulated.
128 devices in a mesh: grp: 2 (over core), row: 8 (over x_lo, y), col: 8 (over z, x_hi).
Axes of the slice: x: 4 (x_hi: 2, x_lo: 2; x = x_hi * 2 + x_lo), y: 4, z: 4, core: 2. Of those that a mesh axis runs over, the one named last changes fastest.
Arguments:
- conserved: float32 [5, 512, 4096], P(None, 'row', 'col'), may hold values from -1 to 5.5, as said below
- displacement: float32 [2, 512, 4096], P(None, ('row', 'col')), may hold values from -0.3 to 0.3
Outputs:
- group_fields: float32 [2, 5, 512, 4096], P('grp', None, 'row', 'col')
Inputs may be any that keep to these rules, and one draw needn't show every extreme that they name: `conserved`: per cell: density and pressure (0.4 times the energy minus the kinetic energy) lie between 1 and 2, both speeds between -0.5 and 0.5, the tracer fraction between 0 and 1.
All inputs are finite; a program needn't handle non-finite values.
Results may differ from a plain program's by a relative error of at most 0.0003.
Values sent between devices are 32-bit elements; how exact they have to be, the bound alone decides.
No kernel may reach another device: no remote copies, remote signals or barrier semaphores. Data moves between devices by JAX's collectives and lax.ppermute only.
A program may use at most 64 MiB of HBM per device.

v0:
```python
import jax
import jax.numpy as jnp
from jax import lax
from jax.sharding import PartitionSpec as P

STEPS = 2
SWEEPS = 4


HEAT_RATIO = 1.4
TIME_STEP = 0.08
GRADIENT_GAIN = 8.0
MONITOR_GAIN = 0.2
RELAXATION = 0.5


def partner(block, axis, apart):
    count = lax.axis_size(axis)
    route = []
    for low in range(count):
        high = low | 1 << apart
        if high != low and high < count:
            route += [(low, high), (high, low)]
    return lax.ppermute(block, axis, route)


def with_halo(cells, sides, width):
    for axis, dim in sides:
        count = lax.axis_size(axis)
        head = lax.slice_in_dim(cells, 0, width, axis=dim)
        tail = lax.slice_in_dim(cells, cells.shape[dim] - width, cells.shape[dim], axis=dim)
        cells = jnp.concatenate(
            [
                lax.ppermute(tail, axis, [(i, (i + 1) % count) for i in range(count)]),
                cells,
                lax.ppermute(head, axis, [((i + 1) % count, i) for i in range(count)]),
            ],
            axis=dim,
        )
    return cells


def minmod(lower_diff, upper_diff):
    smaller = jnp.where(jnp.abs(lower_diff) < jnp.abs(upper_diff), lower_diff, upper_diff)
    return jnp.where(lower_diff * upper_diff > 0.0, smaller, 0.0)


def primitives(fields):
    density = fields[0]
    speed_x = fields[1] / density
    speed_y = fields[2] / density
    pressure = (HEAT_RATIO - 1.0) * (fields[3] - 0.5 * (fields[1] * speed_x + fields[2] * speed_y))
    tracer = fields[4] / density
    return jnp.stack([density, speed_x, speed_y, pressure, tracer])


def normal_flux(states, normal_x, normal_y):
    density, speed_x, speed_y, pressure, tracer = (
        states[0],
        states[1],
        states[2],
        states[3],
        states[4],
    )
    normal_speed = speed_x * normal_x + speed_y * normal_y
    energy = pressure / (HEAT_RATIO - 1.0) + 0.5 * density * (speed_x * speed_x + speed_y * speed_y)
    conserved = jnp.stack([density, density * speed_x, density * speed_y, energy, density * tracer])
    flux_terms = jnp.stack(
        [
            density * normal_speed,
            density * speed_x * normal_speed + pressure * normal_x,
            density * speed_y * normal_speed + pressure * normal_y,
            (energy + pressure) * normal_speed,
            density * tracer * normal_speed,
        ]
    )
    wave_speed = jnp.abs(normal_speed) + jnp.sqrt(HEAT_RATIO * pressure / density) * jnp.sqrt(
        normal_x * normal_x + normal_y * normal_y
    )
    return (conserved, flux_terms, wave_speed)


def rusanov(left_state, right_state, normal_x, normal_y):
    cons_left, flux_left, wave_left = normal_flux(left_state, normal_x, normal_y)
    cons_right, flux_right, wave_right = normal_flux(right_state, normal_x, normal_y)
    wave_speed = jnp.maximum(wave_left, wave_right)
    return 0.5 * (flux_left + flux_right) - 0.5 * wave_speed * (cons_right - cons_left)


def face_states(primitive, along_axis):
    extent = primitive.shape[along_axis]
    differences = lax.slice_in_dim(primitive, 1, extent, axis=along_axis) - lax.slice_in_dim(
        primitive, 0, extent - 1, axis=along_axis
    )
    slopes = minmod(
        lax.slice_in_dim(differences, 0, extent - 2, axis=along_axis),
        lax.slice_in_dim(differences, 1, extent - 1, axis=along_axis),
    )
    left_state = lax.slice_in_dim(
        primitive, 1, extent - 2, axis=along_axis
    ) + 0.5 * lax.slice_in_dim(slopes, 0, extent - 3, axis=along_axis)
    right_state = lax.slice_in_dim(
        primitive, 2, extent - 1, axis=along_axis
    ) - 0.5 * lax.slice_in_dim(slopes, 1, extent - 2, axis=along_axis)
    return (left_state, right_state)


def advance(extended):
    primitive = primitives(extended[:5])
    shift_x = extended[5]
    shift_y = extended[6]
    slope_x_col = 1.0 + 0.5 * (shift_x[1:-1, 2:] - shift_x[1:-1, :-2])
    slope_x_row = 0.5 * (shift_x[2:, 1:-1] - shift_x[:-2, 1:-1])
    slope_y_col = 0.5 * (shift_y[1:-1, 2:] - shift_y[1:-1, :-2])
    slope_y_row = 1.0 + 0.5 * (shift_y[2:, 1:-1] - shift_y[:-2, 1:-1])
    normal_x = 0.5 * (slope_y_row[1:-1, :-1] + slope_y_row[1:-1, 1:])
    normal_y = -0.5 * (slope_x_row[1:-1, :-1] + slope_x_row[1:-1, 1:])
    left_state, right_state = face_states(primitive[:, 2:-2, :], 2)
    col_flux = rusanov(left_state, right_state, normal_x, normal_y)
    normal_x = -0.5 * (slope_y_col[:-1, 1:-1] + slope_y_col[1:, 1:-1])
    normal_y = 0.5 * (slope_x_col[:-1, 1:-1] + slope_x_col[1:, 1:-1])
    left_state, right_state = face_states(primitive[:, :, 2:-2], 1)
    row_flux = rusanov(left_state, right_state, normal_x, normal_y)
    jacobian = (
        slope_x_col[1:-1, 1:-1] * slope_y_row[1:-1, 1:-1]
        - slope_x_row[1:-1, 1:-1] * slope_y_col[1:-1, 1:-1]
    )
    change = col_flux[:, :, 1:] - col_flux[:, :, :-1] + (row_flux[:, 1:, :] - row_flux[:, :-1, :])
    return extended[:5, 2:-2, 2:-2] - TIME_STEP / jacobian * change


def monitor(density, pressure):
    density_col = 0.5 * (density[1:-1, 2:] - density[1:-1, :-2])
    density_row = 0.5 * (density[2:, 1:-1] - density[:-2, 1:-1])
    pressure_col = 0.5 * (pressure[1:-1, 2:] - pressure[1:-1, :-2])
    pressure_row = 0.5 * (pressure[2:, 1:-1] - pressure[:-2, 1:-1])
    strength = GRADIENT_GAIN * (
        density_col * density_col
        + density_row * density_row
        + pressure_col * pressure_col
        + pressure_row * pressure_row
    )
    return 1.0 + MONITOR_GAIN * strength / (1.0 + strength)


def jacobi(shifts, weight):
    center = weight[1:-1, 1:-1]
    east_face = 0.5 * (center + weight[1:-1, 2:])
    west_face = 0.5 * (center + weight[1:-1, :-2])
    north_face = 0.5 * (center + weight[2:, 1:-1])
    south_face = 0.5 * (center + weight[:-2, 1:-1])
    face_total = east_face + west_face + north_face + south_face
    middle = shifts[:, 1:-1, 1:-1]
    beside_all = (
        east_face * shifts[:, 1:-1, 2:]
        + west_face * shifts[:, 1:-1, :-2]
        + north_face * shifts[:, 2:, 1:-1]
        + south_face * shifts[:, :-2, 1:-1]
    )
    source = jnp.stack([east_face - west_face, north_face - south_face])
    target = (beside_all + source) / face_total
    return middle + RELAXATION * (target - middle)


def pair_of(fields):
    primitive = primitives(fields)
    return jnp.stack([primitive[0], primitive[3]])


def on_device(conserved, displacement):
    on_mesh = lax.axis_index("grp") == 1
    column_count = lax.axis_size("col")
    block_rows = conserved.shape[1]
    block_cols = conserved.shape[2]
    slab_rows = displacement.shape[1]

    def to_pieces_block(values):
        return values.reshape(values.shape[0], column_count, slab_rows, block_cols)

    def to_pieces_slab(values):
        return values.reshape(values.shape[0], slab_rows, column_count, block_cols).transpose(
            0, 2, 1, 3
        )

    def from_pieces_block(values):
        return values.reshape(values.shape[0], block_rows, block_cols)

    def from_pieces_slab(values):
        return values.transpose(0, 2, 1, 3).reshape(
            values.shape[0], slab_rows, column_count * block_cols
        )

    def regroup(values):
        return lax.all_to_all(values, "col", split_axis=1, concat_axis=1, tiled=True)

    def only_mesh(worker, fallback, operands):
        return lax.cond(on_mesh, lambda packed: worker(*packed), lambda packed: fallback, operands)

    def slab_extend(values, margin):
        extended = with_halo(values, ((("row", "col"), 1),), margin)
        return jnp.concatenate(
            [extended[:, :, -margin:], extended, extended[:, :, :margin]], axis=2
        )

    pairs_block = pair_of(conserved)
    arrived = regroup(
        jnp.where(on_mesh, to_pieces_block(pairs_block), to_pieces_slab(displacement))
    )
    shifts_block = from_pieces_block(arrived)
    pairs_mesh = from_pieces_slab(arrived)
    shifts_mesh = displacement
    current = conserved
    previous = shifts_mesh
    weight = jnp.zeros(shifts_mesh.shape[1:], jnp.float32)
    for step_index in range(STEPS):
        physics_extended = with_halo(
            jnp.concatenate([current, shifts_block]), (("row", 1), ("col", 2)), 2
        )
        only_fallback = current
        new_state = lax.cond(
            on_mesh,
            lambda packed: only_fallback,
            lambda packed: advance(*packed),
            (physics_extended,),
        )
        shifts = shifts_mesh
        mesh_extended = slab_extend(jnp.concatenate([pairs_mesh, shifts]), 2)
        blank = jnp.zeros((mesh_extended.shape[1] - 2, mesh_extended.shape[2] - 2), jnp.float32)
        weight_cycle = only_mesh(monitor, blank, (mesh_extended[0], mesh_extended[1]))
        rim_shifts = mesh_extended[2:4, 1:-1, 1:-1]
        for sweep_index in range(SWEEPS):
            if sweep_index > 0:
                rim_shifts = slab_extend(shifts, 1)
            shifts = only_mesh(jacobi, shifts, (rim_shifts, weight_cycle))
        mesh_weight = weight_cycle[1:-1, 1:-1]
        weight = mesh_weight
        if step_index + 1 < STEPS:
            new_pairs = pair_of(new_state)
            outgoing = jnp.where(on_mesh, to_pieces_slab(shifts), to_pieces_block(new_pairs))
            arrived = partner(regroup(outgoing), "grp", 0)
            shifts_block = from_pieces_block(arrived)
            pairs_mesh = from_pieces_slab(arrived)
        previous = shifts_mesh
        shifts_mesh = shifts
        current = new_state
    mesh_fields = jnp.stack(
        [
            shifts_mesh[0],
            shifts_mesh[1],
            (shifts_mesh[0] - previous[0]) / TIME_STEP,
            (shifts_mesh[1] - previous[1]) / TIME_STEP,
            weight,
        ]
    )
    mesh_fields = from_pieces_block(regroup(to_pieces_slab(mesh_fields)))
    return jnp.where(on_mesh, mesh_fields, current)[None]


def solution(mesh):
    placed = (P(None, "row", "col"), P(None, ("row", "col"), None))
    return jax.shard_map(
        on_device,
        mesh=mesh,
        in_specs=placed,
        out_specs=P("grp", None, "row", "col"),
        check_vma=False,
    )
```

profile of v0, /device:TPU:0, one launch (start us, length us, event | category | flops | bytes accessed | tf_op | source)
XLA Modules:
  0.0 185.4 jit_solution(14474896401639339898)
XLA Ops:
  2.2 16.4 %all_to_all.15 = f32[2,8,8,512]{3,2,0,1:T(8,128)S(1)} all-to-all(f32[2,8,8,512]{3,2,0,1:T(8,128)S(1)} %copy.13), channel_id=1, replica_groups=mesh['grp'=2,'row'=8,'col'=8] {'col'}, dimensions={1} | all-to-all | bytes 524288 | tf_op jit(solution)/shard_map/all_to_all | solution.py:194
  18.8 3.7 %collective-permute-start.1 = (f32[4,2,4096]{2,1,0:T(2,128)S(1)}, f32[4,2,4096]{2,1,0:T(2,128)S(1)}, u32[]{:S(2)}, u32[]{:S(2)}) collective-permute-start(f32[4,2,4096]{2,1,0:T(2,128)S(1)} %get-tuple-element.352), channel_id=1, source_target_pairs={{1,0},{2,1},{3,2},{4,3},{5,4},{6,5},{7,6},{8,7},{9,8},{10,9},{11,1... | collective-permute-start | bytes 393224 | tf_op jit(solution)/shard_map/ppermute | solution.py:36
  22.6 3.0 %collective-permute-start.9 = (f32[7,2,512]{2,1,0:T(2,128)S(1)}, f32[7,2,512]{2,1,0:T(2,128)S(1)}, u32[]{:S(2)}, u32[]{:S(2)}) collective-permute-start(f32[7,2,512]{2,1,0:T(2,128)S(1)} %get-tuple-element.330), channel_id=1, source_target_pairs={{8,0},{16,8},{24,16},{32,24},{40,32},{48,40},{56,48},{0,56},{9,1},... | collective-permute-start | bytes 86024 | tf_op jit(solution)/shard_map/ppermute | solution.py:36
  26.5 6.7 %collective-permute-done = f32[4,2,4096]{2,1,0:T(2,128)S(1)} collective-permute-done((f32[4,2,4096]{2,1,0:T(2,128)S(1)}, f32[4,2,4096]{2,1,0:T(2,128)S(1)}, u32[]{:S(2)}, u32[]{:S(2)}) %collective-permute-start) | collective-permute-done | bytes 131104 | tf_op jit(solution)/shard_map/ppermute | solution.py:34
  37.4 2.3 %collective-permute-start.2 = (f32[2,1,4096]{2,1,0:T(1,128)S(1)}, f32[2,1,4096]{2,1,0:T(1,128)S(1)}, u32[]{:S(2)}, u32[]{:S(2)}) collective-permute-start(f32[2,1,4096]{2,1,0:T(1,128)S(1)} %get-tuple-element.363), channel_id=1, source_target_pairs={{0,1},{1,2},{2,3},{3,4},{4,5},{5,6},{6,7},{7,8},{8,9},{9,10},{10,1... | collective-permute-start | bytes 98312 | tf_op jit(solution)/shard_map/ppermute | solution.py:34
  41.3 2.2 %collective-permute-start.10 = (f32[7,68,2]{2,1,0:T(8,128)S(1)}, f32[7,68,2]{2,1,0:T(8,128)}, u32[]{:S(2)}, u32[]{:S(2)}) collective-permute-start(f32[7,68,2]{2,1,0:T(8,128)S(1)} %get-tuple-element.325), channel_id=1, source_target_pairs={{0,1},{1,2},{2,3},{3,4},{4,5},{5,6},{6,7},{7,0},{8,9},{9,10},{10,1... | collective-permute-start | bytes 11432 | tf_op jit(solution)/shard_map/ppermute | solution.py:34
  43.5 7.2 %collective-permute-done.3 = f32[2,1,4096]{2,1,0:T(1,128)S(1)} collective-permute-done((f32[2,1,4096]{2,1,0:T(1,128)S(1)}, f32[2,1,4096]{2,1,0:T(1,128)S(1)}, u32[]{:S(2)}, u32[]{:S(2)}) %collective-permute-start.3) | collective-permute-done | bytes 32800 | tf_op jit(solution)/shard_map/ppermute | solution.py:36
  50.7 3.4 %collective-permute-done.2 = f32[2,1,4096]{2,1,0:T(1,128)S(1)} collective-permute-done((f32[2,1,4096]{2,1,0:T(1,128)S(1)}, f32[2,1,4096]{2,1,0:T(1,128)S(1)}, u32[]{:S(2)}, u32[]{:S(2)}) %collective-permute-start.2) | collective-permute-done | bytes 32800 | tf_op jit(solution)/shard_map/ppermute | solution.py:34
  54.6 4.5 %collective-permute-start.5 = (f32[2,1,4096]{2,1,0:T(1,128)S(1)}, f32[2,1,4096]{2,1,0:T(1,128)S(1)}, u32[]{:S(2)}, u32[]{:S(2)}) collective-permute-start(f32[2,1,4096]{2,1,0:T(1,128)S(1)} %get-tuple-element.362), channel_id=1, source_target_pairs={{1,0},{2,1},{3,2},{4,3},{5,4},{6,5},{7,6},{8,7},{9,8},{10,9},{11,1... | collective-permute-start | bytes 98312 | tf_op jit(solution)/shard_map/ppermute | solution.py:36
  60.8 6.8 %conditional.17 = (f32[5,64,512]{2,1,0:T(8,128)S(1)}) conditional(s32[]{:T(128)} %convert_element_type.2, (f32[7,68,516]{2,1,0:T(8,128)S(1)}, f32[5,64,512]{2,1,0:T(8,128)S(1)}) %tuple.239, f32[5,64,512]{2,1,0:T(8,128)S(1)} %copy-done), branch_computations={%region_10.11_spmd, %region_11.12_spmd} | conditional | flops 12940432 | bytes 60802312 | solution.py:220
  69.0 6.7 %collective-permute-start.7 = (f32[2,1,4096]{2,1,0:T(1,128)S(1)}, f32[2,1,4096]{2,1,0:T(1,128)S(1)}, u32[]{:S(2)}, u32[]{:S(2)}) collective-permute-start(f32[2,1,4096]{2,1,0:T(1,128)S(1)} %get-tuple-element.360), channel_id=1, source_target_pairs={{1,0},{2,1},{3,2},{4,3},{5,4},{6,5},{7,6},{8,7},{9,8},{10,9},{11,1... | collective-permute-start | bytes 98312 | tf_op jit(solution)/shard_map/ppermute | solution.py:36
  77.3 7.8 %collective-permute-done.6 = f32[2,1,4096]{2,1,0:T(1,128)S(1)} collective-permute-done((f32[2,1,4096]{2,1,0:T(1,128)S(1)}, f32[2,1,4096]{2,1,0:T(1,128)S(1)}, u32[]{:S(2)}, u32[]{:S(2)}) %collective-permute-start.6) | collective-permute-done | bytes 32800 | tf_op jit(solution)/shard_map/ppermute | solution.py:34
  85.6 11.2 %all_to_all.16 = f32[2,8,8,512]{3,2,0,1:T(8,128)S(1)} all-to-all(f32[2,8,8,512]{3,2,0,1:T(8,128)S(1)} %copy.17), channel_id=1, replica_groups=mesh['grp'=2,'row'=8,'col'=8] {'col'}, dimensions={1} | all-to-all | bytes 524288 | tf_op jit(solution)/shard_map/all_to_all | solution.py:194
  100.0 2.1 %collective-permute-start.13 = (f32[4,2,4096]{2,1,0:T(2,128)S(1)}, f32[4,2,4096]{2,1,0:T(2,128)S(1)}, u32[]{:S(2)}, u32[]{:S(2)}) collective-permute-start(f32[4,2,4096]{2,1,0:T(2,128)S(1)} %get-tuple-element.343), channel_id=1, source_target_pairs={{0,1},{1,2},{2,3},{3,4},{4,5},{5,6},{6,7},{7,8},{8,9},{9,10},{10,1... | collective-permute-start | bytes 393224 | tf_op jit(solution)/shard_map/ppermute | solution.py:34
  102.1 4.3 %collective-permute-done.14 = f32[4,2,4096]{2,1,0:T(2,128)S(1)} collective-permute-done((f32[4,2,4096]{2,1,0:T(2,128)S(1)}, f32[4,2,4096]{2,1,0:T(2,128)S(1)}, u32[]{:S(2)}, u32[]{:S(2)}) %collective-permute-start.14) | collective-permute-done | bytes 131104 | tf_op jit(solution)/shard_map/ppermute | solution.py:36
  106.4 4.6 %collective-permute-done.13 = f32[4,2,4096]{2,1,0:T(2,128)S(1)} collective-permute-done((f32[4,2,4096]{2,1,0:T(2,128)S(1)}, f32[4,2,4096]{2,1,0:T(2,128)S(1)}, u32[]{:S(2)}, u32[]{:S(2)}) %collective-permute-start.13) | collective-permute-done | bytes 131104 | tf_op jit(solution)/shard_map/ppermute | solution.py:34
  115.1 3.5 %collective-permute-start.15 = (f32[2,1,4096]{2,1,0:T(1,128)S(1)}, f32[2,1,4096]{2,1,0:T(1,128)S(1)}, u32[]{:S(2)}, u32[]{:S(2)}) collective-permute-start(f32[2,1,4096]{2,1,0:T(1,128)S(1)} %get-tuple-element.357), channel_id=1, source_target_pairs={{0,1},{1,2},{2,3},{3,4},{4,5},{5,6},{6,7},{7,8},{8,9},{9,10},{10,1... | collective-permute-start | bytes 98312 | tf_op jit(solution)/shard_map/ppermute | solution.py:34
  118.7 1.9 %collective-permute-done.16 = f32[2,1,4096]{2,1,0:T(1,128)S(1)} collective-permute-done((f32[2,1,4096]{2,1,0:T(1,128)S(1)}, f32[2,1,4096]{2,1,0:T(1,128)S(1)}, u32[]{:S(2)}, u32[]{:S(2)}) %collective-permute-start.16) | collective-permute-done | bytes 32800 | tf_op jit(solution)/shard_map/ppermute | solution.py:36
  120.5 4.0 %collective-permute-done.15 = f32[2,1,4096]{2,1,0:T(1,128)S(1)} collective-permute-done((f32[2,1,4096]{2,1,0:T(1,128)S(1)}, f32[2,1,4096]{2,1,0:T(1,128)S(1)}, u32[]{:S(2)}, u32[]{:S(2)}) %collective-permute-start.15) | collective-permute-done | bytes 32800 | tf_op jit(solution)/shard_map/ppermute | solution.py:34
  125.2 3.5 %collective-permute-start.17 = (f32[2,1,4096]{2,1,0:T(1,128)S(1)}, f32[2,1,4096]{2,1,0:T(1,128)S(1)}, u32[]{:S(2)}, u32[]{:S(2)}) collective-permute-start(f32[2,1,4096]{2,1,0:T(1,128)S(1)} %get-tuple-element.355), channel_id=1, source_target_pairs={{0,1},{1,2},{2,3},{3,4},{4,5},{5,6},{6,7},{7,8},{8,9},{9,10},{10,1... | collective-permute-start | bytes 98312 | tf_op jit(solution)/shard_map/ppermute | solution.py:34
  128.7 1.9 %collective-permute-done.18 = f32[2,1,4096]{2,1,0:T(1,128)S(1)} collective-permute-done((f32[2,1,4096]{2,1,0:T(1,128)S(1)}, f32[2,1,4096]{2,1,0:T(1,128)S(1)}, u32[]{:S(2)}, u32[]{:S(2)}) %collective-permute-start.18) | collective-permute-done | bytes 32800 | tf_op jit(solution)/shard_map/ppermute | solution.py:36
  130.6 4.0 %collective-permute-done.17 = f32[2,1,4096]{2,1,0:T(1,128)S(1)} collective-permute-done((f32[2,1,4096]{2,1,0:T(1,128)S(1)}, f32[2,1,4096]{2,1,0:T(1,128)S(1)}, u32[]{:S(2)}, u32[]{:S(2)}) %collective-permute-start.17) | collective-permute-done | bytes 32800 | tf_op jit(solution)/shard_map/ppermute | solution.py:34
  135.3 3.5 %collective-permute-start.19 = (f32[2,1,4096]{2,1,0:T(1,128)S(1)}, f32[2,1,4096]{2,1,0:T(1,128)S(1)}, u32[]{:S(2)}, u32[]{:S(2)}) collective-permute-start(f32[2,1,4096]{2,1,0:T(1,128)S(1)} %get-tuple-element.353), channel_id=1, source_target_pairs={{0,1},{1,2},{2,3},{3,4},{4,5},{5,6},{6,7},{7,8},{8,9},{9,10},{10,1... | collective-permute-start | bytes 98312 | tf_op jit(solution)/shard_map/ppermute | solution.py:34
  138.8 1.9 %collective-permute-done.20 = f32[2,1,4096]{2,1,0:T(1,128)S(1)} collective-permute-done((f32[2,1,4096]{2,1,0:T(1,128)S(1)}, f32[2,1,4096]{2,1,0:T(1,128)S(1)}, u32[]{:S(2)}, u32[]{:S(2)}) %collective-permute-start.20) | collective-permute-done | bytes 32800 | tf_op jit(solution)/shard_map/ppermute | solution.py:36
  140.7 5.9 %collective-permute-done.19 = f32[2,1,4096]{2,1,0:T(1,128)S(1)} collective-permute-done((f32[2,1,4096]{2,1,0:T(1,128)S(1)}, f32[2,1,4096]{2,1,0:T(1,128)S(1)}, u32[]{:S(2)}, u32[]{:S(2)}) %collective-permute-start.19) | collective-permute-done | bytes 32800 | tf_op jit(solution)/shard_map/ppermute | solution.py:34
  148.7 3.5 %all-to-all-start.2 = ((f32[5,8,8,512]{3,2,0,1:T(8,128)}), f32[5,8,8,512]{3,2,0,1:T(8,128)S(1)}, u32[]{:S(2)}, u32[]{:S(2)}) async-start(f32[5,8,8,512]{3,2,0,1:T(8,128)} %copy.20), calls=%async_computation.2 | async-start | bytes 1310720 | tf_op jit(solution)/shard_map/all_to_all | solution.py:194
  152.4 2.0 %collective-permute-start.21 = (f32[7,2,512]{2,1,0:T(2,128)S(1)}, f32[7,2,512]{2,1,0:T(2,128)S(1)}, u32[]{:S(2)}, u32[]{:S(2)}) collective-permute-start(f32[7,2,512]{2,1,0:T(2,128)S(1)} %get-tuple-element.327), channel_id=1, source_target_pairs={{0,8},{8,16},{16,24},{24,32},{32,40},{40,48},{48,56},{56,0},{1,9},... | collective-permute-start | bytes 86024 | tf_op jit(solution)/shard_map/ppermute | solution.py:34
  154.4 2.9 %collective-permute-done.22 = f32[7,2,512]{2,1,0:T(2,128)S(1)} collective-permute-done((f32[7,2,512]{2,1,0:T(2,128)S(1)}, f32[7,2,512]{2,1,0:T(2,128)S(1)}, u32[]{:S(2)}, u32[]{:S(2)}) %collective-permute-start.22) | collective-permute-done | bytes 28704 | tf_op jit(solution)/shard_map/ppermute | solution.py:36
  158.6 5.6 %collective-permute-start.24 = (f32[7,68,2]{2,1,0:T(8,128)S(1)}, f32[7,68,2]{2,1,0:T(8,128)S(1)}, u32[]{:S(2)}, u32[]{:S(2)}) collective-permute-start(f32[7,68,2]{2,1,0:T(8,128)S(1)} %get-tuple-element.324), channel_id=1, source_target_pairs={{1,0},{2,1},{3,2},{4,3},{5,4},{6,5},{7,6},{0,7},{9,8},{10,9},{11,1... | collective-permute-start | bytes 11432 | tf_op jit(solution)/shard_map/ppermute | solution.py:36
  164.2 4.9 %collective-permute-done.24 = f32[7,68,2]{2,1,0:T(8,128)S(1)} collective-permute-done((f32[7,68,2]{2,1,0:T(8,128)S(1)}, f32[7,68,2]{2,1,0:T(8,128)S(1)}, u32[]{:S(2)}, u32[]{:S(2)}) %collective-permute-start.24) | collective-permute-done | bytes 3840 | tf_op jit(solution)/shard_map/ppermute | solution.py:36
  169.1 7.8 %collective-permute-done.23 = f32[7,68,2]{2,1,0:T(8,128)S(1)} collective-permute-done((f32[7,68,2]{2,1,0:T(8,128)S(1)}, f32[7,68,2]{2,1,0:T(8,128)S(1)}, u32[]{:S(2)}, u32[]{:S(2)}) %collective-permute-start.23) | collective-permute-done | bytes 3840 | tf_op jit(solution)/shard_map/ppermute | solution.py:34
  177.5 6.9 %conditional.23 = (f32[5,64,512]{2,1,0:T(8,128)S(1)}) conditional(s32[]{:T(128)} %convert_element_type.2, (f32[7,68,516]{2,1,0:T(8,128)S(1)}, f32[5,64,512]{2,1,0:T(8,128)S(1)}) %tuple.90, f32[5,64,512]{2,1,0:T(8,128)S(1)} %get-tuple-element.376), branch_computations={%region_22.23_spmd, %region_23.24_spmd} | conditional | flops 12940432 | bytes 60802312 | solution.py:220
  (192 shorter events, 41.5 us)
Async XLA Ops:
  18.6 3.9 %copy-start = (f32[5,64,512]{2,1,0:T(8,128)S(1)}, f32[5,64,512]{2,1,0:T(8,128)}, u32[]{:S(2)}) copy-start(f32[5,64,512]{2,1,0:T(8,128)} %param.26) | copy-start | bytes 1966084
  18.8 7.7 %collective-permute-start.1 = (f32[4,2,4096]{2,1,0:T(2,128)S(1)}, f32[4,2,4096]{2,1,0:T(2,128)S(1)}, u32[]{:S(2)}, u32[]{:S(2)}) collective-permute-start(f32[4,2,4096]{2,1,0:T(2,128)S(1)} %get-tuple-element.352), channel_id=1, source_target_pairs={{1,0},{2,1},{3,2},{4,3},{5,4},{6,5},{7,6},{8,7},{9,8},{10,9},{11,1... | collective-permute-start | bytes 393224 | tf_op jit(solution)/shard_map/ppermute | solution.py:36
  22.5 10.7 %collective-permute-start = (f32[4,2,4096]{2,1,0:T(2,128)S(1)}, f32[4,2,4096]{2,1,0:T(2,128)S(1)}, u32[]{:S(2)}, u32[]{:S(2)}) collective-permute-start(f32[4,2,4096]{2,1,0:T(2,128)S(1)} %get-tuple-element.351), channel_id=1, source_target_pairs={{0,1},{1,2},{2,3},{3,4},{4,5},{5,6},{6,7},{7,8},{8,9},{9,10},{10,1... | collective-permute-start | bytes 393224 | tf_op jit(solution)/shard_map/ppermute | solution.py:34
  22.6 17.1 %collective-permute-start.9 = (f32[7,2,512]{2,1,0:T(2,128)S(1)}, f32[7,2,512]{2,1,0:T(2,128)S(1)}, u32[]{:S(2)}, u32[]{:S(2)}) collective-permute-start(f32[7,2,512]{2,1,0:T(2,128)S(1)} %get-tuple-element.330), channel_id=1, source_target_pairs={{8,0},{16,8},{24,16},{32,24},{40,32},{48,40},{56,48},{0,56},{9,1},... | collective-permute-start | bytes 86024 | tf_op jit(solution)/shard_map/ppermute | solution.py:36
  25.6 14.2 %collective-permute-start.8 = (f32[7,2,512]{2,1,0:T(2,128)S(1)}, f32[7,2,512]{2,1,0:T(2,128)S(1)}, u32[]{:S(2)}, u32[]{:S(2)}) collective-permute-start(f32[7,2,512]{2,1,0:T(2,128)S(1)} %get-tuple-element.329), channel_id=1, source_target_pairs={{0,8},{8,16},{16,24},{24,32},{32,40},{40,48},{48,56},{56,0},{1,9},... | collective-permute-start | bytes 86024 | tf_op jit(solution)/shard_map/ppermute | solution.py:34
  33.4 1.0 copy-start.1
  36.1 14.6 %collective-permute-start.3 = (f32[2,1,4096]{2,1,0:T(1,128)S(1)}, f32[2,1,4096]{2,1,0:T(1,128)S(1)}, u32[]{:S(2)}, u32[]{:S(2)}) collective-permute-start(f32[2,1,4096]{2,1,0:T(1,128)S(1)} %get-tuple-element.364), channel_id=1, source_target_pairs={{1,0},{2,1},{3,2},{4,3},{5,4},{6,5},{7,6},{8,7},{9,8},{10,9},{11,1... | collective-permute-start | bytes 98312 | tf_op jit(solution)/shard_map/ppermute | solution.py:36
  37.4 16.7 %collective-permute-start.2 = (f32[2,1,4096]{2,1,0:T(1,128)S(1)}, f32[2,1,4096]{2,1,0:T(1,128)S(1)}, u32[]{:S(2)}, u32[]{:S(2)}) collective-permute-start(f32[2,1,4096]{2,1,0:T(1,128)S(1)} %get-tuple-element.363), channel_id=1, source_target_pairs={{0,1},{1,2},{2,3},{3,4},{4,5},{5,6},{6,7},{7,8},{8,9},{9,10},{10,1... | collective-permute-start | bytes 98312 | tf_op jit(solution)/shard_map/ppermute | solution.py:34
  39.9 19.3 %collective-permute-start.11 = (f32[7,68,2]{2,1,0:T(8,128)S(1)}, f32[7,68,2]{2,1,0:T(8,128)}, u32[]{:S(2)}, u32[]{:S(2)}) collective-permute-start(f32[7,68,2]{2,1,0:T(8,128)S(1)} %get-tuple-element.326), channel_id=1, source_target_pairs={{1,0},{2,1},{3,2},{4,3},{5,4},{6,5},{7,6},{0,7},{9,8},{10,9},{11,1... | collective-permute-start | bytes 11432 | tf_op jit(solution)/shard_map/ppermute | solution.py:36
  41.3 17.9 %collective-permute-start.10 = (f32[7,68,2]{2,1,0:T(8,128)S(1)}, f32[7,68,2]{2,1,0:T(8,128)}, u32[]{:S(2)}, u32[]{:S(2)}) collective-permute-start(f32[7,68,2]{2,1,0:T(8,128)S(1)} %get-tuple-element.325), channel_id=1, source_target_pairs={{0,1},{1,2},{2,3},{3,4},{4,5},{5,6},{6,7},{7,0},{8,9},{9,10},{10,1... | collective-permute-start | bytes 11432 | tf_op jit(solution)/shard_map/ppermute | solution.py:34
  54.6 13.0 %collective-permute-start.5 = (f32[2,1,4096]{2,1,0:T(1,128)S(1)}, f32[2,1,4096]{2,1,0:T(1,128)S(1)}, u32[]{:S(2)}, u32[]{:S(2)}) collective-permute-start(f32[2,1,4096]{2,1,0:T(1,128)S(1)} %get-tuple-element.362), channel_id=1, source_target_pairs={{1,0},{2,1},{3,2},{4,3},{5,4},{6,5},{7,6},{8,7},{9,8},{10,9},{11,1... | collective-permute-start | bytes 98312 | tf_op jit(solution)/shard_map/ppermute | solution.py:36
  59.2 9.3 %collective-permute-start.4 = (f32[2,1,4096]{2,1,0:T(1,128)S(1)}, f32[2,1,4096]{2,1,0:T(1,128)S(1)}, u32[]{:S(2)}, u32[]{:S(2)}) collective-permute-start(f32[2,1,4096]{2,1,0:T(1,128)S(1)} %get-tuple-element.361), channel_id=1, source_target_pairs={{0,1},{1,2},{2,3},{3,4},{4,5},{5,6},{6,7},{7,8},{8,9},{9,10},{10,1... | collective-permute-start | bytes 98312 | tf_op jit(solution)/shard_map/ppermute | solution.py:34
  69.0 8.3 %collective-permute-start.7 = (f32[2,1,4096]{2,1,0:T(1,128)S(1)}, f32[2,1,4096]{2,1,0:T(1,128)S(1)}, u32[]{:S(2)}, u32[]{:S(2)}) collective-permute-start(f32[2,1,4096]{2,1,0:T(1,128)S(1)} %get-tuple-element.360), channel_id=1, source_target_pairs={{1,0},{2,1},{3,2},{4,3},{5,4},{6,5},{7,6},{8,7},{9,8},{10,9},{11,1... | collective-permute-start | bytes 98312 | tf_op jit(solution)/shard_map/ppermute | solution.py:36
  75.7 9.4 %collective-permute-start.6 = (f32[2,1,4096]{2,1,0:T(1,128)S(1)}, f32[2,1,4096]{2,1,0:T(1,128)S(1)}, u32[]{:S(2)}, u32[]{:S(2)}) collective-permute-start(f32[2,1,4096]{2,1,0:T(1,128)S(1)} %get-tuple-element.359), channel_id=1, source_target_pairs={{0,1},{1,2},{2,3},{3,4},{4,5},{5,6},{6,7},{7,8},{8,9},{9,10},{10,1... | collective-permute-start | bytes 98312 | tf_op jit(solution)/shard_map/ppermute | solution.py:34
  96.8 1.6 collective-permute-start.12
  98.5 7.9 %collective-permute-start.14 = (f32[4,2,4096]{2,1,0:T(2,128)S(1)}, f32[4,2,4096]{2,1,0:T(2,128)S(1)}, u32[]{:S(2)}, u32[]{:S(2)}) collective-permute-start(f32[4,2,4096]{2,1,0:T(2,128)S(1)} %get-tuple-element.344), channel_id=1, source_target_pairs={{1,0},{2,1},{3,2},{4,3},{5,4},{6,5},{7,6},{8,7},{9,8},{10,9},{11,1... | collective-permute-start | bytes 393224 | tf_op jit(solution)/shard_map/ppermute | solution.py:36
  100.0 11.0 %collective-permute-start.13 = (f32[4,2,4096]{2,1,0:T(2,128)S(1)}, f32[4,2,4096]{2,1,0:T(2,128)S(1)}, u32[]{:S(2)}, u32[]{:S(2)}) collective-permute-start(f32[4,2,4096]{2,1,0:T(2,128)S(1)} %get-tuple-element.343), channel_id=1, source_target_pairs={{0,1},{1,2},{2,3},{3,4},{4,5},{5,6},{6,7},{7,8},{8,9},{9,10},{10,1... | collective-permute-start | bytes 393224 | tf_op jit(solution)/shard_map/ppermute | solution.py:34
  111.3 1.0 copy-start.2
  115.1 5.5 %collective-permute-start.16 = (f32[2,1,4096]{2,1,0:T(1,128)S(1)}, f32[2,1,4096]{2,1,0:T(1,128)S(1)}, u32[]{:S(2)}, u32[]{:S(2)}) collective-permute-start(f32[2,1,4096]{2,1,0:T(1,128)S(1)} %get-tuple-element.358), channel_id=1, source_target_pairs={{1,0},{2,1},{3,2},{4,3},{5,4},{6,5},{7,6},{8,7},{9,8},{10,9},{11,1... | collective-permute-start | bytes 98312 | tf_op jit(solution)/shard_map/ppermute | solution.py:36
  115.1 9.4 %collective-permute-start.15 = (f32[2,1,4096]{2,1,0:T(1,128)S(1)}, f32[2,1,4096]{2,1,0:T(1,128)S(1)}, u32[]{:S(2)}, u32[]{:S(2)}) collective-permute-start(f32[2,1,4096]{2,1,0:T(1,128)S(1)} %get-tuple-element.357), channel_id=1, source_target_pairs={{0,1},{1,2},{2,3},{3,4},{4,5},{5,6},{6,7},{7,8},{8,9},{9,10},{10,1... | collective-permute-start | bytes 98312 | tf_op jit(solution)/shard_map/ppermute | solution.py:34
  125.1 5.5 %collective-permute-start.18 = (f32[2,1,4096]{2,1,0:T(1,128)S(1)}, f32[2,1,4096]{2,1,0:T(1,128)S(1)}, u32[]{:S(2)}, u32[]{:S(2)}) collective-permute-start(f32[2,1,4096]{2,1,0:T(1,128)S(1)} %get-tuple-element.356), channel_id=1, source_target_pairs={{1,0},{2,1},{3,2},{4,3},{5,4},{6,5},{7,6},{8,7},{9,8},{10,9},{11,1... | collective-permute-start | bytes 98312 | tf_op jit(solution)/shard_map/ppermute | solution.py:36
  125.2 9.4 %collective-permute-start.17 = (f32[2,1,4096]{2,1,0:T(1,128)S(1)}, f32[2,1,4096]{2,1,0:T(1,128)S(1)}, u32[]{:S(2)}, u32[]{:S(2)}) collective-permute-start(f32[2,1,4096]{2,1,0:T(1,128)S(1)} %get-tuple-element.355), channel_id=1, source_target_pairs={{0,1},{1,2},{2,3},{3,4},{4,5},{5,6},{6,7},{7,8},{8,9},{9,10},{10,1... | collective-permute-start | bytes 98312 | tf_op jit(solution)/shard_map/ppermute | solution.py:34
  135.2 5.5 %collective-permute-start.20 = (f32[2,1,4096]{2,1,0:T(1,128)S(1)}, f32[2,1,4096]{2,1,0:T(1,128)S(1)}, u32[]{:S(2)}, u32[]{:S(2)}) collective-permute-start(f32[2,1,4096]{2,1,0:T(1,128)S(1)} %get-tuple-element.354), channel_id=1, source_target_pairs={{1,0},{2,1},{3,2},{4,3},{5,4},{6,5},{7,6},{8,7},{9,8},{10,9},{11,1... | collective-permute-start | bytes 98312 | tf_op jit(solution)/shard_map/ppermute | solution.py:36
  135.3 11.3 %collective-permute-start.19 = (f32[2,1,4096]{2,1,0:T(1,128)S(1)}, f32[2,1,4096]{2,1,0:T(1,128)S(1)}, u32[]{:S(2)}, u32[]{:S(2)}) collective-permute-start(f32[2,1,4096]{2,1,0:T(1,128)S(1)} %get-tuple-element.353), channel_id=1, source_target_pairs={{0,1},{1,2},{2,3},{3,4},{4,5},{5,6},{6,7},{7,8},{8,9},{9,10},{10,1... | collective-permute-start | bytes 98312 | tf_op jit(solution)/shard_map/ppermute | solution.py:34
  148.7 35.7 %all-to-all-start.2 = ((f32[5,8,8,512]{3,2,0,1:T(8,128)}), f32[5,8,8,512]{3,2,0,1:T(8,128)S(1)}, u32[]{:S(2)}, u32[]{:S(2)}) async-start(f32[5,8,8,512]{3,2,0,1:T(8,128)} %copy.20), calls=%async_computation.2 | async-start | bytes 1310720 | tf_op jit(solution)/shard_map/all_to_all | solution.py:194
  152.3 5.0 %collective-permute-start.22 = (f32[7,2,512]{2,1,0:T(2,128)S(1)}, f32[7,2,512]{2,1,0:T(2,128)S(1)}, u32[]{:S(2)}, u32[]{:S(2)}) collective-permute-start(f32[7,2,512]{2,1,0:T(2,128)S(1)} %get-tuple-element.328), channel_id=1, source_target_pairs={{8,0},{16,8},{24,16},{32,24},{40,32},{48,40},{56,48},{0,56},{9,1},... | collective-permute-start | bytes 86024 | tf_op jit(solution)/shard_map/ppermute | solution.py:36
  152.4 6.0 %collective-permute-start.21 = (f32[7,2,512]{2,1,0:T(2,128)S(1)}, f32[7,2,512]{2,1,0:T(2,128)S(1)}, u32[]{:S(2)}, u32[]{:S(2)}) collective-permute-start(f32[7,2,512]{2,1,0:T(2,128)S(1)} %get-tuple-element.327), channel_id=1, source_target_pairs={{0,8},{8,16},{16,24},{24,32},{32,40},{40,48},{48,56},{56,0},{1,9},... | collective-permute-start | bytes 86024 | tf_op jit(solution)/shard_map/ppermute | solution.py:34
  158.6 10.5 %collective-permute-start.24 = (f32[7,68,2]{2,1,0:T(8,128)S(1)}, f32[7,68,2]{2,1,0:T(8,128)S(1)}, u32[]{:S(2)}, u32[]{:S(2)}) collective-permute-start(f32[7,68,2]{2,1,0:T(8,128)S(1)} %get-tuple-element.324), channel_id=1, source_target_pairs={{1,0},{2,1},{3,2},{4,3},{5,4},{6,5},{7,6},{0,7},{9,8},{10,9},{11,1... | collective-permute-start | bytes 11432 | tf_op jit(solution)/shard_map/ppermute | solution.py:36
  164.2 12.7 %collective-permute-start.23 = (f32[7,68,2]{2,1,0:T(8,128)S(1)}, f32[7,68,2]{2,1,0:T(8,128)S(1)}, u32[]{:S(2)}, u32[]{:S(2)}) collective-permute-start(f32[7,68,2]{2,1,0:T(8,128)S(1)} %get-tuple-element.323), channel_id=1, source_target_pairs={{0,1},{1,2},{2,3},{3,4},{4,5},{5,6},{6,7},{7,0},{8,9},{9,10},{10,1... | collective-permute-start | bytes 11432 | tf_op jit(solution)/shard_map/ppermute | solution.py:34
where the time goes:
time: 186 us; the launch traced here: 185 us
  waiting for transfers between devices  75.3 us (40%)
  starting transfers between devices  50.8 us (27%)
  blocking collectives  27.6 us (15%)
  other arithmetic  18.6 us (10%)
  local copies, waits for them, and re-layouts  11.2 us (6%)
    ppermute x12, waiting for transfers between devices, with_halo(): lax.ppermute(tail, axis, [(i, (i + 1) % count) for i in range(count)])  46.3 us
    ppermute x12, starting transfers between devices, with_halo(): lax.ppermute(head, axis, [((i + 1) % count, i) for i in range(count)])  28.1 us
    all_to_all x2, blocking collectives, regroup(): lax.all_to_all(values, 'col', split_axis=1, concat_axis=1, tiled=True)  27.6 us
    ppermute x12, waiting for transfers between devices, with_halo(): lax.ppermute(head, axis, [((i + 1) % count, i) for i in range(count)])  27.5 us
    ppermute x12, starting transfers between devices, with_halo(): lax.ppermute(tail, axis, [(i, (i + 1) % count) for i in range(count)])  19.1 us
    concatenate x8, local copies, waits for them, and re-layouts, slab_extend(): jnp.concatenate([extended[:, :, -margin:], extended, extended[:, :, :marg...  5.05 us
  transfers between devices with their start and end apart: 26, of which 20 were waited for; matrix products, arithmetic and copies ran while one was open for 10% of the time, Pallas kernels for 0%

commit v1 on v0

v1 whole, which is shorter than its diff:
```python
import jax
import jax.numpy as jnp
from jax import lax
from jax.experimental import pallas as pl
from jax.experimental.pallas import tpu as pltpu
from jax.sharding import PartitionSpec as P

SWEEPS = 4
HEAT_RATIO = 1.4
TIME_STEP = 0.08
GRADIENT_GAIN = 8.0
MONITOR_GAIN = 0.2

BAND = 11
EXT = 8 * BAND
PAD = 12
ROW_HALO = 9
DISP_HALO = 8
EDGE = 128


def next_col(x):
    return pltpu.roll(x, x.shape[1] - 1, 1)


def prev_col(x):
    return pltpu.roll(x, 1, 1)


def next_band(x):
    return pltpu.roll(x, 7, 0)


def prev_band(x):
    return pltpu.roll(x, 1, 0)


def minmod(a, b):
    return jnp.maximum(jnp.minimum(a, b), 0.0) + jnp.minimum(jnp.maximum(a, b), 0.0)


def twice_flux(left, right, nx, ny):
    n2 = HEAT_RATIO * (nx * nx + ny * ny)

    def one(state):
        rho, u, v, p, q = state
        mu, mv, mq = rho * u, rho * v, rho * q
        energy = (1.0 / (HEAT_RATIO - 1.0)) * p + 0.5 * (mu * u + mv * v)
        speed = u * nx + v * ny
        x = p * n2
        wave = jnp.abs(speed) + x * lax.rsqrt(jnp.maximum(x * rho, 1e-30))
        flux = (rho * speed, mu * speed + p * nx, mv * speed + p * ny, (energy + p) * speed, mq * speed)
        return (rho, mu, mv, energy, mq), flux, wave

    cl, fl, sl = one(left)
    cr, fr, sr = one(right)
    s = jnp.maximum(sl, sr)
    return [fl[k] + fr[k] - s * (cr[k] - cl[k]) for k in range(5)]


def each_row(body, unroll=1):
    lax.fori_loop(0, BAND, lambda t, carry: (body(t), carry)[1], 0, unroll=unroll)


def to_primitives(load, prim):
    for t in range(BAND):
        rho, mx, my, en, tr = load(t)
        inv = 1.0 / rho
        u, v = mx * inv, my * inv
        p = (HEAT_RATIO - 1.0) * (en - 0.5 * (mx * u + my * v))
        for k, x in enumerate((rho, u, v, p, tr * inv)):
            prim[k, t + 2] = x
    for k in range(5):
        prim[k, 0] = prev_band(prim[k, BAND])
        prim[k, 1] = prev_band(prim[k, BAND + 1])
        prim[k, BAND + 2] = next_band(prim[k, 2])
        prim[k, BAND + 3] = next_band(prim[k, 3])


def wrap_rows(ref, *lead):
    ref[(*lead, 0)] = prev_band(ref[(*lead, BAND)])
    ref[(*lead, BAND + 1)] = next_band(ref[(*lead, 1)])


def to_weight(prim, weight):
    def body(t):
        g = 0.0
        for k in (0, 3):
            x = prim[k, t + 2]
            a = next_col(x) - prev_col(x)
            b = prim[k, t + 3] - prim[k, t + 1]
            g = g + (a * a + b * b)
        g = (0.25 * GRADIENT_GAIN) * g
        weight[t + 1] = (1.0 + MONITOR_GAIN) - MONITOR_GAIN / (1.0 + g)

    each_row(body)
    wrap_rows(weight)


def to_coefs(weight, coef):
    def body(t):
        c = weight[t + 1]
        e = c + next_col(c)
        w = c + prev_col(c)
        n = c + weight[t + 2]
        s = c + weight[t]
        k = 0.5 / ((e + w) + (n + s))
        coef[0, t] = e * k
        coef[1, t] = w * k
        coef[2, t] = n * k
        coef[3, t] = s * k

    each_row(body)


def sweep(src, dst, coef):
    def body(t):
        he, hw, hn, hs = coef[0, t], coef[1, t], coef[2, t], coef[3, t]
        for k in range(2):
            x = src[k, t + 1]
            source = he - hw if k == 0 else hn - hs
            beside = he * next_col(x) + hw * prev_col(x) + (hn * src[k, t + 2] + hs * src[k, t])
            dst[k, t + 1] = (0.5 * x + source) + beside

    each_row(body)
    for k in range(2):
        wrap_rows(dst, k)


def to_metrics(disp, face, slope):
    def body(t):
        dx, dy = disp[0, t + 1], disp[1, t + 1]
        xc = 1.0 + 0.5 * (next_col(dx) - prev_col(dx))
        yc = 0.5 * (next_col(dy) - prev_col(dy))
        xr = 0.5 * (disp[0, t + 2] - disp[0, t])
        yr = 1.0 + 0.5 * (disp[1, t + 2] - disp[1, t])
        face[0, t] = 0.5 * (yr + next_col(yr))
        face[1, t] = -0.5 * (xr + next_col(xr))
        face[2, t] = (0.5 * TIME_STEP) / (xc * yr - xr * yc)
        slope[0, t] = xc
        slope[1, t] = yc

    each_row(body)
    for k in range(2):
        slope[k, BAND] = next_band(slope[k, 0])


def to_changes(prim, half, face, slope, colch, rowfl):
    def slopes(t):
        for k in range(5):
            x = prim[k, t + 2]
            half[k, t] = minmod(0.5 * (x - prim[k, t + 1]), 0.5 * (prim[k, t + 3] - x))

    each_row(slopes)
    for k in range(5):
        half[k, BAND] = next_band(half[k, 0])

    def body(t):
        left, right = [], []
        for k in range(5):
            x = prim[k, t + 2]
            d = 0.5 * (next_col(x) - x)
            h = minmod(d, prev_col(d))
            left.append(x + h)
            right.append(next_col(x - h))
        flux = twice_flux(left, right, face[0, t], face[1, t])
        for k in range(5):
            colch[k, t] = flux[k] - prev_col(flux[k])

    each_row(body)

    def rbody(t):
        nx = -0.5 * (slope[1, t] + slope[1, t + 1])
        ny = 0.5 * (slope[0, t] + slope[0, t + 1])
        left = [prim[k, t + 2] + half[k, t] for k in range(5)]
        right = [prim[k, t + 3] - half[k, t + 1] for k in range(5)]
        flux = twice_flux(left, right, nx, ny)
        for k in range(5):
            rowfl[k, t + 1] = flux[k]

    each_row(rbody)
    for k in range(5):
        rowfl[k, 0] = prev_band(rowfl[k, BAND])


def core(u_ref, tile_ref, top_ref, bot_ref, dblk_ref, dtop_ref, dbot_ref, out_ref,
         ext, prim, half, face, slope, colch, rowfl, weight, coef, da, db, cons, flat):
    rows, cols = u_ref.shape[1], u_ref.shape[2]
    wide = cols + EDGE
    tiles = wide // EDGE

    def place(k, row, value):
        for j in range(value.shape[1] // EDGE):
            ext[k, j, row:row + value.shape[0], :] = value[:, EDGE * j:EDGE * (j + 1)]

    for k in range(5):
        place(k, PAD, u_ref[k])
        ext[k, tiles - 1, PAD:PAD + rows, :] = tile_ref[k]
        place(k, PAD - ROW_HALO, top_ref[k, 16 - ROW_HALO:16])
        place(k, PAD + rows, bot_ref[k, :ROW_HALO])
    for k in range(2):
        for c in range(dblk_ref.shape[0]):
            place(5 + k, PAD + 8 * c, dblk_ref[c, k])
        place(5 + k, PAD - DISP_HALO, dtop_ref[k])
        place(5 + k, PAD + rows, dbot_ref[k])

    def band(k, t):
        return jnp.concatenate([ext[k, j, pl.ds(t, 8, stride=BAND), :] for j in range(tiles)], 1)

    to_primitives(lambda t: [band(k, t) for k in range(5)], prim)
    for k in range(2):
        for t in range(BAND):
            da[k, t + 1] = band(5 + k, t)
        wrap_rows(da, k)
    to_metrics(da, face, slope)
    to_weight(prim, weight)
    to_coefs(weight, coef)
    src, dst = da, db
    for _ in range(SWEEPS):
        sweep(src, dst, coef)
        src, dst = dst, src
    to_changes(prim, half, face, slope, colch, rowfl)
    for t in range(BAND):
        scale = face[2, t]
        for k in range(5):
            cons[k, t] = band(k, t) - scale * (colch[k, t] + (rowfl[k, t + 1] - rowfl[k, t]))
    to_primitives(lambda t: [cons[k, t] for k in range(5)], prim)

    def put(k, t, x):
        for j in range(tiles - 1):
            flat[k, j, pl.ds(t, 8, stride=BAND), :] = x[:, EDGE * j:EDGE * (j + 1)]

    group = lax.axis_index("grp")

    @pl.when(group == 0)
    def _():
        to_metrics(da, face, slope)
        to_changes(prim, half, face, slope, colch, rowfl)
        for t in range(BAND):
            scale = face[2, t]
            for k in range(5):
                put(k, t, cons[k, t] - scale * (colch[k, t] + (rowfl[k, t + 1] - rowfl[k, t])))

    @pl.when(group == 1)
    def _():
        for t in range(BAND):
            for k in range(2):
                cons[k, t] = da[k, t + 1]
        to_weight(prim, weight)
        to_coefs(weight, coef)
        src, dst = da, db
        for _ in range(SWEEPS):
            sweep(src, dst, coef)
            src, dst = dst, src
        for t in range(BAND):
            for k in range(2):
                put(k, t, da[k, t + 1])
                put(k + 2, t, (da[k, t + 1] - cons[k, t]) * (1.0 / TIME_STEP))
            put(4, t, weight[t + 1])

    for k in range(5):
        for j in range(tiles - 1):
            out_ref[0, k, :, EDGE * j:EDGE * (j + 1)] = flat[k, j, PAD:PAD + rows, :]


def compute(u, tile, top, bot, dblk, dtop, dbot):
    rows, cols = u.shape[1], u.shape[2]
    wide = cols + EDGE
    vec = lambda *lead: pltpu.VMEM((*lead, 8, wide), jnp.float32)
    return pl.pallas_call(
        core,
        out_shape=jax.ShapeDtypeStruct((1, 5, rows, cols), jnp.float32),
        in_specs=[pl.BlockSpec(memory_space=pltpu.VMEM)] * 7,
        out_specs=pl.BlockSpec(memory_space=pltpu.VMEM),
        scratch_shapes=[
            pltpu.VMEM((7, wide // EDGE, EXT, EDGE), jnp.float32),
            vec(5, BAND + 4), vec(5, BAND + 1), vec(3, BAND), vec(2, BAND + 1),
            vec(5, BAND), vec(5, BAND + 1), vec(BAND + 2), vec(4, BAND),
            vec(2, BAND + 2), vec(2, BAND + 2), vec(5, BAND),
            pltpu.VMEM((5, cols // EDGE, EXT, EDGE), jnp.float32),
        ],
        name="euler_mesh",
    )(u, tile, top, bot, dblk, dtop, dbot)


def shift(x, axis, step):
    count = lax.axis_size(axis)
    return lax.ppermute(x, axis, [(i, (i + step) % count) for i in range(count)])


def on_device(conserved, displacement):
    cols = conserved.shape[2]
    parts = lax.axis_size("col")
    lane = lax.broadcasted_iota(jnp.int32, (1, 1, EDGE), 2)
    from_left = shift(conserved[:, :, cols - EDGE:], "col", 1)
    from_right = shift(conserved[:, :, :EDGE], "col", -1)
    pieces = displacement.reshape(2, displacement.shape[1], parts, cols).transpose(2, 0, 1, 3)
    right = jnp.roll(pieces, -1, 0)[..., :EDGE]
    left = jnp.roll(pieces, 1, 0)[..., cols - EDGE:]
    pieces = jnp.concatenate([pieces, jnp.where(lane < EDGE // 2, right, left)], -1)
    dblk = lax.all_to_all(pieces, "col", 0, 0, tiled=True)
    tile = jnp.where(lane < EDGE // 2, from_right, from_left)
    bottom = jnp.concatenate([conserved[:, -16:], tile[:, -16:]], 2)
    upper = jnp.concatenate([conserved[:, :16], tile[:, :16]], 2)
    top = shift(bottom, "row", 1)
    dtop = shift(dblk[-1], "row", 1)
    bot = shift(upper, "row", -1)
    dbot = shift(dblk[0], "row", -1)
    return compute(conserved, tile, top, bot, dblk, dtop, dbot)


def solution(mesh):
    placed = (P(None, "row", "col"), P(None, ("row", "col"), None))
    return jax.shard_map(
        on_device,
        mesh=mesh,
        in_specs=placed,
        out_specs=P("grp", None, "row", "col"),
        check_vma=False,
    )
```

time: 186 us -> 57.1 us (0.31)
  waiting for transfers between devices: 75.3 us -> 10.3 us
  starting transfers between devices: 50.8 us -> 20.6 us
  blocking collectives: 27.6 us -> 0 us
  Pallas kernels: 0 us -> 21.8 us
  other arithmetic: 18.6 us -> 0.82 us
  local copies, waits for them, and re-layouts: 11.2 us -> 3.14 us
    ppermute x25 -> x6, waiting for transfers between devices: 75.3 us -> 6.19 us  [shift(): lax.ppermute(x, axis, [(i, (i + step) % count) for i in range(count)])]
    ppermute x25 -> x6, starting transfers between devices: 47.3 us -> 15.9 us  [shift(): lax.ppermute(x, axis, [(i, (i + step) % count) for i in range(count)])]
    all_to_all x2 -> x0, blocking collectives: 27.6 us -> none  [regroup(): lax.all_to_all(values, 'col', split_axis=1, concat_axis=1, tiled=True)]
    pallas_call x0 -> x1, Pallas kernels: none -> 21.8 us  [compute(): pl.pallas_call(core, out_shape=jax.ShapeDtypeStruct((1, 5, rows, cols), j...]
    concatenate x9 -> x0, local copies, waits for them, and re-layouts: 5.07 us -> none  [the longest x8 5.05 us: slab_extend(): jnp.concatenate([extended[:, :, -margin:], extended, extended[:, :, :marg...]
    all_to_all x1, waiting for transfers between devices: 0.01 us -> 4.1 us  [on_device(): dblk = lax.all_to_all(pieces, 'col', 0, 0, tiled=True)]
    sub x10 -> x0, other arithmetic: 3.74 us -> none  [the longest x4 1.54 us: face_states(): lax.slice_in_dim(primitive, 1, extent, axis=along_axis)]
    cond x46 -> x0, other arithmetic: 2.43 us -> none
  transfers between devices with their start and end apart: 26 -> 7, of which waited for: 20 -> 4; matrix products, arithmetic and copies ran while one was open for 10% -> 2% of each run, Pallas kernels for 0% -> 0%
where the time goes in v1:
time: 57.1 us; the launch traced here: 56.8 us
  Pallas kernels  21.8 us (38%)
  starting transfers between devices  20.6 us (36%)
  waiting for transfers between devices  10.3 us (18%)
  local copies, waits for them, and re-layouts  3.14 us (5%)
  other arithmetic  0.82 us (1%)
    pallas_call x1, Pallas kernels, compute(): pl.pallas_call(core, out_shape=jax.ShapeDtypeStruct((1, 5, rows, cols), j...  21.8 us
    ppermute x6, starting transfers between devices, shift(): lax.ppermute(x, axis, [(i, (i + step) % count) for i in range(count)])  15.9 us
    ppermute x6, waiting for transfers between devices, shift(): lax.ppermute(x, axis, [(i, (i + step) % count) for i in range(count)])  6.19 us
    all_to_all x1, starting transfers between devices, on_device(): dblk = lax.all_to_all(pieces, 'col', 0, 0, tiled=True)  4.72 us
    all_to_all x1, waiting for transfers between devices, on_device(): dblk = lax.all_to_all(pieces, 'col', 0, 0, tiled=True)  4.1 us
    unnamed x16, local copies, waits for them, and re-layouts  1.97 us
  transfers between devices with their start and end apart: 7, of which 4 were waited for; matrix products, arithmetic and copies ran while one was open for 2% of the time, Pallas kernels for 0%

profile of v1, /device:TPU:0, one launch (start us, length us, event | category | flops | bytes accessed | tf_op | source)
XLA Modules:
  0.0 56.8 jit_solution(11709400600593410947)
XLA Ops:
  0.0 0.0 copy-start.3
  0.0 1.1 %fusion.2 = (f32[5,64,128]{2,1,0:T(8,128)S(1)}, f32[5,64,128]{2,1,0:T(8,128)S(1)}) fusion(f32[5,64,512]{2,1,0:T(8,128)} %u_ref.1), kind=kLoop, calls=%fused_computation.12 | loop fusion | bytes 655360 | tf_op jit(solution)/shard_map/slice | solution.py:295
  1.1 3.2 %collective-permute-start.1 = (f32[5,64,128]{2,1,0:T(8,128)S(1)}, f32[5,64,128]{2,1,0:T(8,128)S(1)}, u32[]{:S(2)}, u32[]{:S(2)}) collective-permute-start(f32[5,64,128]{2,1,0:T(8,128)S(1)} %get-tuple-element.7), channel_id=1, source_target_pairs={{0,1},{1,2},{2,3},{3,4},{4,5},{5,6},{6,7},{7,0},{8,9},{9,10},{10,1... | collective-permute-start | bytes 491528 | tf_op jit(solution)/shard_map/ppermute | solution.py:288
  4.2 3.6 %collective-permute-start = (f32[5,64,128]{2,1,0:T(8,128)S(1)}, f32[5,64,128]{2,1,0:T(8,128)S(1)}, u32[]{:S(2)}, u32[]{:S(2)}) collective-permute-start(f32[5,64,128]{2,1,0:T(8,128)S(1)} %get-tuple-element.8), channel_id=1, source_target_pairs={{0,7},{1,0},{2,1},{3,2},{4,3},{5,4},{6,5},{7,6},{8,15},{9,8},{10,9... | collective-permute-start | bytes 491528 | tf_op jit(solution)/shard_map/ppermute | solution.py:288
  7.8 0.0 copy-done.3
  7.9 0.0 copy-start
  7.9 0.7 %pad_maximum_fusion = f32[8,2,8,640]{3,2,1,0:T(8,128)} fusion(f32[8,2,8,128]{3,2,1,0:T(8,128)S(1)} %fusion, f32[8,2,8,512]{3,2,1,0:T(8,128)S(1)} %bitcast.13), kind=kLoop, calls=%fused_computation | loop fusion | flops 81920 | bytes 655360 | tf_op jit(solution)/shard_map/concatenate | solution.py:300
  8.7 4.7 %all-to-all-start = ((f32[8,2,8,640]{3,2,1,0:T(8,128)}), f32[8,2,8,640]{3,2,1,0:T(8,128)S(1)}, u32[]{:S(2)}, u32[]{:S(2)}) async-start(f32[8,2,8,640]{3,2,1,0:T(8,128)} %pad_maximum_fusion), calls=%async_computation | async-start | bytes 655360 | tf_op jit(solution)/shard_map/all_to_all | solution.py:301
  13.4 0.0 copy-done
  13.4 0.0 collective-permute-done.1
  13.5 0.1 collective-permute-done
  13.6 0.0 copy-start.2
  13.6 0.6 %copy-done.2 = f32[5,64,128]{2,1,0:T(8,128)} copy-done((f32[5,64,128]{2,1,0:T(8,128)}, f32[5,64,128]{2,1,0:T(8,128)S(1)}, u32[]{:S(2)}) %copy-start.2) | copy-done | bytes 163864
  14.2 1.6 %collective-permute-start.2 = (f32[5,16,640]{2,1,0:T(8,128)S(1)}, f32[5,16,640]{2,1,0:T(8,128)S(1)}, u32[]{:S(2)}, u32[]{:S(2)}) collective-permute-start(f32[5,16,640]{2,1,0:T(8,128)S(1)} %pad_maximum_fusion.1), channel_id=1, source_target_pairs={{0,8},{8,16},{16,24},{24,32},{32,40},{40,48},{48,56},{56,0},{1,9},... | collective-permute-start | bytes 614408 | tf_op jit(solution)/shard_map/ppermute | solution.py:288
  15.8 2.6 %collective-permute-start.3 = (f32[5,16,640]{2,1,0:T(8,128)S(1)}, f32[5,16,640]{2,1,0:T(8,128)S(1)}, u32[]{:S(2)}, u32[]{:S(2)}) collective-permute-start(f32[5,16,640]{2,1,0:T(8,128)S(1)} %pad_maximum_fusion.2), channel_id=1, source_target_pairs={{0,56},{8,0},{16,8},{24,16},{32,24},{40,32},{48,40},{56,48},{1,57}... | collective-permute-start | bytes 614408 | tf_op jit(solution)/shard_map/ppermute | solution.py:288
  18.4 4.1 %all-to-all-done.dblk_ref = f32[8,2,8,640]{3,2,1,0:T(8,128)S(1)} async-done(((f32[8,2,8,640]{3,2,1,0:T(8,128)}), f32[8,2,8,640]{3,2,1,0:T(8,128)S(1)}, u32[]{:S(2)}, u32[]{:S(2)}) %all-to-all-start) | async-done | bytes 327712 | tf_op jit(solution)/shard_map/all_to_all | solution.py:301
  22.5 0.0 copy-start.1
  22.6 4.9 %collective-permute-start.5 = (f32[2,8,640]{2,1,0:T(8,128)S(1)}, f32[2,8,640]{2,1,0:T(8,128)S(1)}, u32[]{:S(2)}, u32[]{:S(2)}) collective-permute-start(f32[2,8,640]{2,1,0:T(8,128)S(1)} %get-tuple-element.9), channel_id=1, source_target_pairs={{0,56},{8,0},{16,8},{24,16},{32,24},{40,32},{48,40},{56,48},{1,57}... | collective-permute-start | bytes 122888 | tf_op jit(solution)/shard_map/ppermute | solution.py:288
  27.5 0.0 collective-permute-start.4
  27.5 1.7 %collective-permute-done.5.dbot_ref = f32[2,8,640]{2,1,0:T(8,128)S(1)} collective-permute-done((f32[2,8,640]{2,1,0:T(8,128)S(1)}, f32[2,8,640]{2,1,0:T(8,128)S(1)}, u32[]{:S(2)}, u32[]{:S(2)}) %collective-permute-start.5) | collective-permute-done | bytes 40992 | tf_op jit(solution)/shard_map/ppermute | solution.py:288
  29.2 0.0 copy-start.6
  29.2 4.4 %collective-permute-done.4.dtop_ref = f32[2,8,640]{2,1,0:T(8,128)S(1)} collective-permute-done((f32[2,8,640]{2,1,0:T(8,128)S(1)}, f32[2,8,640]{2,1,0:T(8,128)S(1)}, u32[]{:S(2)}, u32[]{:S(2)}) %collective-permute-start.4) | collective-permute-done | bytes 40992 | tf_op jit(solution)/shard_map/ppermute | solution.py:288
  33.6 0.0 copy-start.7
  33.6 0.0 collective-permute-done.2.top_ref
  33.6 0.0 copy-start.4
  33.6 0.0 collective-permute-done.3.bot_ref
  33.6 0.0 copy-done.1
  33.6 0.0 copy-done.6
  33.6 0.6 %copy-done.7 = f32[2,8,640]{2,1,0:T(8,128)} copy-done((f32[2,8,640]{2,1,0:T(8,128)}, f32[2,8,640]{2,1,0:T(8,128)S(1)}, u32[]{:S(2)}) %copy-start.7) | copy-done | bytes 40984
  34.2 0.1 copy-done.4
  34.3 0.7 %copy-done.5 = f32[5,16,640]{2,1,0:T(8,128)} copy-done((f32[5,16,640]{2,1,0:T(8,128)}, f32[5,16,640]{2,1,0:T(8,128)S(1)}, u32[]{:S(2)}) %copy-start.5) | copy-done | bytes 204824
  35.0 21.8 %euler_mesh.1 = f32[1,5,64,512]{3,2,1,0:T(8,128)} custom-call(f32[5,64,512]{2,1,0:T(8,128)} %u_ref.1, f32[5,64,128]{2,1,0:T(8,128)} %copy-done.2, f32[5,16,640]{2,1,0:T(8,128)} %copy-done.4, f32[5,16,640]{2,1,0:T(8,128)} %copy-done.5, f32[8,2,8,640]{3,2,1,0:T(8,128)} %copy-done.1, f32[2,8,640]{2,1,0:T(8,128)} %copy-done.7, f32[2,8,640]{2,1,0:T(8,128)} %copy-done.6), custom_call_target="tpu_custom_call" | custom-call | tf_op jit(solution)/shard_map/euler_mesh/pallas_call | solution.py:270
  (12 shorter events, 0.2 us)
Async XLA Ops:
  0.0 7.8 %copy-start.3 = (f32[2,8,4096]{2,1,0:T(8,128)S(1)}, f32[2,8,4096]{2,1,0:T(8,128)}, u32[]{:S(2)}) copy-start(f32[2,8,4096]{2,1,0:T(8,128)} %param.3) | copy-start | bytes 786436
  1.1 12.4 %collective-permute-start.1 = (f32[5,64,128]{2,1,0:T(8,128)S(1)}, f32[5,64,128]{2,1,0:T(8,128)S(1)}, u32[]{:S(2)}, u32[]{:S(2)}) collective-permute-start(f32[5,64,128]{2,1,0:T(8,128)S(1)} %get-tuple-element.7), channel_id=1, source_target_pairs={{0,1},{1,2},{2,3},{3,4},{4,5},{5,6},{6,7},{7,0},{8,9},{9,10},{10,1... | collective-permute-start | bytes 491528 | tf_op jit(solution)/shard_map/ppermute | solution.py:288
  4.2 9.3 %collective-permute-start = (f32[5,64,128]{2,1,0:T(8,128)S(1)}, f32[5,64,128]{2,1,0:T(8,128)S(1)}, u32[]{:S(2)}, u32[]{:S(2)}) collective-permute-start(f32[5,64,128]{2,1,0:T(8,128)S(1)} %get-tuple-element.8), channel_id=1, source_target_pairs={{0,7},{1,0},{2,1},{3,2},{4,3},{5,4},{6,5},{7,6},{8,15},{9,8},{10,9... | collective-permute-start | bytes 491528 | tf_op jit(solution)/shard_map/ppermute | solution.py:288
  7.9 5.5 %copy-start = (f32[5,64,512]{2,1,0:T(8,128)S(1)}, f32[5,64,512]{2,1,0:T(8,128)}, u32[]{:S(2)}) copy-start(f32[5,64,512]{2,1,0:T(8,128)} %u_ref.1) | copy-start | bytes 1966084
  8.7 13.9 %all-to-all-start = ((f32[8,2,8,640]{3,2,1,0:T(8,128)}), f32[8,2,8,640]{3,2,1,0:T(8,128)S(1)}, u32[]{:S(2)}, u32[]{:S(2)}) async-start(f32[8,2,8,640]{3,2,1,0:T(8,128)} %pad_maximum_fusion), calls=%async_computation | async-start | bytes 655360 | tf_op jit(solution)/shard_map/all_to_all | solution.py:301
  13.6 0.7 %copy-start.2 = (f32[5,64,128]{2,1,0:T(8,128)}, f32[5,64,128]{2,1,0:T(8,128)S(1)}, u32[]{:S(2)}) copy-start(f32[5,64,128]{2,1,0:T(8,128)S(1)} %broadcast_select_fusion.tile_ref) | copy-start | bytes 491524
  14.2 19.4 %collective-permute-start.2 = (f32[5,16,640]{2,1,0:T(8,128)S(1)}, f32[5,16,640]{2,1,0:T(8,128)S(1)}, u32[]{:S(2)}, u32[]{:S(2)}) collective-permute-start(f32[5,16,640]{2,1,0:T(8,128)S(1)} %pad_maximum_fusion.1), channel_id=1, source_target_pairs={{0,8},{8,16},{16,24},{24,32},{32,40},{40,48},{48,56},{56,0},{1,9},... | collective-permute-start | bytes 614408 | tf_op jit(solution)/shard_map/ppermute | solution.py:288
  15.8 17.8 %collective-permute-start.3 = (f32[5,16,640]{2,1,0:T(8,128)S(1)}, f32[5,16,640]{2,1,0:T(8,128)S(1)}, u32[]{:S(2)}, u32[]{:S(2)}) collective-permute-start(f32[5,16,640]{2,1,0:T(8,128)S(1)} %pad_maximum_fusion.2), channel_id=1, source_target_pairs={{0,56},{8,0},{16,8},{24,16},{32,24},{40,32},{48,40},{56,48},{1,57}... | collective-permute-start | bytes 614408 | tf_op jit(solution)/shard_map/ppermute | solution.py:288
  22.5 11.1 %copy-start.1 = (f32[8,2,8,640]{3,2,1,0:T(8,128)}, f32[8,2,8,640]{3,2,1,0:T(8,128)S(1)}, u32[]{:S(2)}) copy-start(f32[8,2,8,640]{3,2,1,0:T(8,128)S(1)} %all-to-all-done.dblk_ref) | copy-start | bytes 983044
  22.6 6.6 %collective-permute-start.5 = (f32[2,8,640]{2,1,0:T(8,128)S(1)}, f32[2,8,640]{2,1,0:T(8,128)S(1)}, u32[]{:S(2)}, u32[]{:S(2)}) collective-permute-start(f32[2,8,640]{2,1,0:T(8,128)S(1)} %get-tuple-element.9), channel_id=1, source_target_pairs={{0,56},{8,0},{16,8},{24,16},{32,24},{40,32},{48,40},{56,48},{1,57}... | collective-permute-start | bytes 122888 | tf_op jit(solution)/shard_map/ppermute | solution.py:288
  27.5 6.1 %collective-permute-start.4 = (f32[2,8,640]{2,1,0:T(8,128)S(1)}, f32[2,8,640]{2,1,0:T(8,128)S(1)}, u32[]{:S(2)}, u32[]{:S(2)}) collective-permute-start(f32[2,8,640]{2,1,0:T(8,128)S(1)} %get-tuple-element.10), channel_id=1, source_target_pairs={{0,8},{8,16},{16,24},{24,32},{32,40},{40,48},{48,56},{56,0},{1,9},... | collective-permute-start | bytes 122888 | tf_op jit(solution)/shard_map/ppermute | solution.py:288
  29.2 4.5 %copy-start.6 = (f32[2,8,640]{2,1,0:T(8,128)}, f32[2,8,640]{2,1,0:T(8,128)S(1)}, u32[]{:S(2)}) copy-start(f32[2,8,640]{2,1,0:T(8,128)S(1)} %collective-permute-done.5.dbot_ref) | copy-start | bytes 122884
  33.6 0.6 %copy-start.7 = (f32[2,8,640]{2,1,0:T(8,128)}, f32[2,8,640]{2,1,0:T(8,128)S(1)}, u32[]{:S(2)}) copy-start(f32[2,8,640]{2,1,0:T(8,128)S(1)} %collective-permute-done.4.dtop_ref) | copy-start | bytes 122884
  33.6 0.7 %copy-start.4 = (f32[5,16,640]{2,1,0:T(8,128)}, f32[5,16,640]{2,1,0:T(8,128)S(1)}, u32[]{:S(2)}) copy-start(f32[5,16,640]{2,1,0:T(8,128)S(1)} %collective-permute-done.2.top_ref) | copy-start | bytes 614404
  34.3 0.7 %copy-start.5 = (f32[5,16,640]{2,1,0:T(8,128)}, f32[5,16,640]{2,1,0:T(8,128)S(1)}, u32[]{:S(2)}) copy-start(f32[5,16,640]{2,1,0:T(8,128)S(1)} %collective-permute-done.3.bot_ref) | copy-start | bytes 614404

commit v2 on v1

v2 whole, which is shorter than its diff:
```python
import jax
import jax.numpy as jnp
from jax import lax
from jax.experimental import pallas as pl
from jax.experimental.pallas import tpu as pltpu
from jax.sharding import PartitionSpec as P

SWEEPS = 4
HEAT_RATIO = 1.4
TIME_STEP = 0.08
GRADIENT_GAIN = 8.0
MONITOR_GAIN = 0.2

BAND = 10
EXT = 8 * BAND
PAD = 8
EDGE = 128
SLOT = 16


def next_col(x):
    return pltpu.roll(x, x.shape[1] - 1, 1)


def prev_col(x):
    return pltpu.roll(x, 1, 1)


def next_band(x):
    return pltpu.roll(x, 7, 0)


def prev_band(x):
    return pltpu.roll(x, 1, 0)


def minmod(a, b):
    return jnp.maximum(jnp.minimum(a, b), 0.0) + jnp.minimum(jnp.maximum(a, b), 0.0)


def twice_flux(left, right, nx, ny):
    n2 = HEAT_RATIO * (nx * nx + ny * ny)

    def one(state):
        rho, u, v, p, q = state
        mu, mv, mq = rho * u, rho * v, rho * q
        energy = (1.0 / (HEAT_RATIO - 1.0)) * p + 0.5 * (mu * u + mv * v)
        speed = u * nx + v * ny
        x = p * n2
        wave = jnp.abs(speed) + x * lax.rsqrt(jnp.maximum(x * rho, 1e-30))
        flux = (rho * speed, mu * speed + p * nx, mv * speed + p * ny, (energy + p) * speed, mq * speed)
        return (rho, mu, mv, energy, mq), flux, wave

    cl, fl, sl = one(left)
    cr, fr, sr = one(right)
    s = jnp.maximum(sl, sr)
    return [fl[k] + fr[k] - s * (cr[k] - cl[k]) for k in range(5)]


def each_row(body, unroll):
    def steps(i, carry):
        for n in range(unroll):
            body(i * unroll + n)
        return carry

    if unroll >= BAND:
        for t in range(BAND):
            body(t)
    else:
        lax.fori_loop(0, BAND // unroll, steps, 0)


def primitives_of(rho, mx, my, en, tr):
    inv = 1.0 / rho
    u, v = mx * inv, my * inv
    p = (HEAT_RATIO - 1.0) * (en - 0.5 * (mx * u + my * v))
    return rho, u, v, p, tr * inv


def wrap_prim(prim):
    for k in range(5):
        prim[k, 0] = prev_band(prim[k, BAND])
        prim[k, 1] = prev_band(prim[k, BAND + 1])
        prim[k, BAND + 2] = next_band(prim[k, 2])
        prim[k, BAND + 3] = next_band(prim[k, 3])


def wrap_rows(ref, *lead):
    ref[(*lead, 0)] = prev_band(ref[(*lead, BAND)])
    ref[(*lead, BAND + 1)] = next_band(ref[(*lead, 1)])


def to_weight(prim, weight):
    def body(t):
        g = 0.0
        for k in (0, 3):
            x = prim[k, t + 2]
            a = next_col(x) - prev_col(x)
            b = prim[k, t + 3] - prim[k, t + 1]
            g = g + (a * a + b * b)
        g = (0.25 * GRADIENT_GAIN) * g
        weight[t + 1] = (1.0 + MONITOR_GAIN) - MONITOR_GAIN / (1.0 + g)

    each_row(body, U_WEIGHT)
    wrap_rows(weight)


def to_coefs(weight, coef):
    def body(t):
        c = weight[t + 1]
        e = c + next_col(c)
        w = c + prev_col(c)
        n = c + weight[t + 2]
        s = c + weight[t]
        k = 0.5 / ((e + w) + (n + s))
        coef[0, t] = e * k
        coef[1, t] = w * k
        coef[2, t] = n * k
        coef[3, t] = s * k

    each_row(body, U_COEF)


def sweep(src, dst, coef):
    def body(t):
        he, hw, hn, hs = coef[0, t], coef[1, t], coef[2, t], coef[3, t]
        for k in range(2):
            x = src[k, t + 1]
            source = he - hw if k == 0 else hn - hs
            beside = he * next_col(x) + hw * prev_col(x) + (hn * src[k, t + 2] + hs * src[k, t])
            dst[k, t + 1] = (0.5 * x + source) + beside

    each_row(body, U_SWEEP)
    for k in range(2):
        wrap_rows(dst, k)


def to_metrics(disp, face, slope):
    def body(t):
        dx, dy = disp[0, t + 1], disp[1, t + 1]
        xc = 1.0 + 0.5 * (next_col(dx) - prev_col(dx))
        yc = 0.5 * (next_col(dy) - prev_col(dy))
        xr = 0.5 * (disp[0, t + 2] - disp[0, t])
        yr = 1.0 + 0.5 * (disp[1, t + 2] - disp[1, t])
        face[0, t] = 0.5 * (yr + next_col(yr))
        face[1, t] = -0.5 * (xr + next_col(xr))
        face[2, t] = (0.5 * TIME_STEP) / (xc * yr - xr * yc)
        slope[0, t] = xc
        slope[1, t] = yc

    each_row(body, U_METRIC)
    for k in range(2):
        slope[k, BAND] = next_band(slope[k, 0])


def to_fluxes(prim, half, side, face, slope, colfl, rowfl):
    def slopes(t):
        for k in range(5):
            x = prim[k, t + 2]
            half[k, t] = minmod(0.5 * (x - prim[k, t + 1]), 0.5 * (prim[k, t + 3] - x))
            d = 0.5 * (next_col(x) - x)
            h = minmod(d, prev_col(d))
            side[k, t] = x + h
            side[5 + k, t] = next_col(x - h)

    each_row(slopes, U_SLOPE)
    for k in range(5):
        half[k, BAND] = next_band(half[k, 0])
    wide = prim.shape[3]

    def fluxes(t):
        for j in range(wide // EDGE):
            at = slice(EDGE * j, EDGE * (j + 1))
            left = [side[k, t, :, at] for k in range(5)]
            right = [side[5 + k, t, :, at] for k in range(5)]
            flux = twice_flux(left, right, face[0, t, :, at], face[1, t, :, at])
            for k in range(5):
                colfl[k, t, :, at] = flux[k]
            nx = -0.5 * (slope[1, t, :, at] + slope[1, t + 1, :, at])
            ny = 0.5 * (slope[0, t, :, at] + slope[0, t + 1, :, at])
            left = [prim[k, t + 2, :, at] + half[k, t, :, at] for k in range(5)]
            right = [prim[k, t + 3, :, at] - half[k, t + 1, :, at] for k in range(5)]
            flux = twice_flux(left, right, nx, ny)
            for k in range(5):
                rowfl[k, t + 1, :, at] = flux[k]

    each_row(fluxes, U_FLUX)
    for k in range(5):
        rowfl[k, 0] = prev_band(rowfl[k, BAND])


def change(k, t, face, colfl, rowfl):
    c = colfl[k, t]
    return face[2, t] * ((c - prev_col(c)) + (rowfl[k, t + 1] - rowfl[k, t]))


def unpack_edges(left, right, k):
    lane = lax.broadcasted_iota(jnp.int32, left.shape, 1)
    a = pltpu.roll(right, (EDGE - SLOT * k) % EDGE, 1)
    b = pltpu.roll(left, (EDGE - SLOT - SLOT * k) % EDGE, 1)
    return jnp.where(lane < EDGE // 2, a, b)


def core(u_ref, left_ref, right_ref, dblk_ref, top_ref, bot_ref, out_ref,
         ext, prim, half, side, face, slope, colfl, rowfl, weight, coef, da, db, cons, flat):
    rows, cols = u_ref.shape[1], u_ref.shape[2]
    tiles = cols // EDGE + 1

    def place(k, row, value):
        for j in range(value.shape[1] // EDGE):
            ext[k, j, row:row + value.shape[0], :] = value[:, EDGE * j:EDGE * (j + 1)]

    left, right = left_ref[...], right_ref[...]
    for k in range(5):
        place(k, PAD, u_ref[k])
        ext[k, tiles - 1, PAD:PAD + rows, :] = unpack_edges(left, right, k)
    for k in range(2):
        for c in range(dblk_ref.shape[0]):
            place(5 + k, PAD + 8 * c, dblk_ref[c, k])
    for k in range(7):
        place(k, 0, top_ref[k])
        place(k, PAD + rows, bot_ref[k])

    def band(k, t):
        return jnp.concatenate([ext[k, j, pl.ds(t, 8, stride=BAND), :] for j in range(tiles)], 1)

    for t in range(BAND):
        for k, x in enumerate(primitives_of(*[band(k, t) for k in range(5)])):
            prim[k, t + 2] = x
    wrap_prim(prim)
    sub = lax.broadcasted_iota(jnp.int32, (8, cols + EDGE), 0)
    for ref, at, hit in ((top_ref, 1, 0), (bot_ref, BAND + 2, 7)):
        outer = [jnp.broadcast_to(ref[7, k:k + 1], (8, cols + EDGE)) for k in range(4)]
        extra = primitives_of(*outer, outer[0])
        for k in (0, 3):
            prim[k, at] = jnp.where(sub == hit, extra[k], prim[k, at])
    for k in range(2):
        for t in range(BAND):
            da[k, t + 1] = band(5 + k, t)
        wrap_rows(da, k)
    to_metrics(da, face, slope)
    to_weight(prim, weight)
    to_coefs(weight, coef)
    src, dst = da, db
    for _ in range(SWEEPS):
        sweep(src, dst, coef)
        src, dst = dst, src
    to_fluxes(prim, half, side, face, slope, colfl, rowfl)
    for t in range(BAND):
        new = [band(k, t) - change(k, t, face, colfl, rowfl) for k in range(5)]
        for k in range(5):
            cons[k, t] = new[k]
        for k, x in enumerate(primitives_of(*new)):
            prim[k, t + 2] = x
    wrap_prim(prim)

    def put(k, t, x):
        for j in range(tiles - 1):
            flat[k, j, pl.ds(t, 8, stride=BAND), :] = x[:, EDGE * j:EDGE * (j + 1)]

    group = lax.axis_index("grp")

    @pl.when(group == 0)
    def _():
        to_metrics(da, face, slope)
        to_fluxes(prim, half, side, face, slope, colfl, rowfl)
        for t in range(BAND):
            for k in range(5):
                put(k, t, cons[k, t] - change(k, t, face, colfl, rowfl))

    @pl.when(group == 1)
    def _():
        for t in range(BAND):
            for k in range(2):
                cons[k, t] = da[k, t + 1]
        to_weight(prim, weight)
        to_coefs(weight, coef)
        src, dst = da, db
        for _ in range(SWEEPS):
            sweep(src, dst, coef)
            src, dst = dst, src
        for t in range(BAND):
            for k in range(2):
                put(k, t, da[k, t + 1])
                put(k + 2, t, (da[k, t + 1] - cons[k, t]) * (1.0 / TIME_STEP))
            put(4, t, weight[t + 1])

    for k in range(5):
        for j in range(tiles - 1):
            out_ref[0, k, :, EDGE * j:EDGE * (j + 1)] = flat[k, j, PAD:PAD + rows, :]


U_WEIGHT = U_COEF = U_SWEEP = U_METRIC = U_SLOPE = 5
U_FLUX = 1


def compute(u, left, right, dblk, top, bot):
    rows, cols = u.shape[1], u.shape[2]
    wide = cols + EDGE
    vec = lambda *lead: pltpu.VMEM((*lead, 8, wide), jnp.float32)
    return pl.pallas_call(
        core,
        out_shape=jax.ShapeDtypeStruct((1, 5, rows, cols), jnp.float32),
        in_specs=[pl.BlockSpec(memory_space=pltpu.VMEM)] * 6,
        out_specs=pl.BlockSpec(memory_space=pltpu.VMEM),
        scratch_shapes=[
            pltpu.VMEM((7, wide // EDGE, EXT, EDGE), jnp.float32),
            vec(5, BAND + 4), vec(5, BAND + 1), vec(10, BAND), vec(3, BAND), vec(2, BAND + 1),
            vec(5, BAND), vec(5, BAND + 1), vec(BAND + 2), vec(4, BAND),
            vec(2, BAND + 2), vec(2, BAND + 2), vec(5, BAND),
            pltpu.VMEM((5, cols // EDGE, EXT, EDGE), jnp.float32),
        ],
        name="euler_mesh",
    )(u, left, right, dblk, top, bot)


def pack(first_ref, last_ref, disp_ref, left_ref, right_ref, piece_ref):
    lane = lax.broadcasted_iota(jnp.int32, left_ref.shape, 1)
    left = right = None
    for k in range(5):
        a = pltpu.roll(first_ref[k], SLOT * k, 1) if k else first_ref[k]
        b = pltpu.roll(last_ref[k], (SLOT + SLOT * k) % EDGE, 1)
        left = a if left is None else jnp.where(lane < SLOT * k, left, a)
        right = b if right is None else jnp.where(lane < SLOT * k, right, b)
    left_ref[...] = left
    right_ref[...] = right
    parts = piece_ref.shape[0]
    cols = piece_ref.shape[3] - EDGE
    lane = lax.broadcasted_iota(jnp.int32, (disp_ref.shape[1], EDGE), 1)
    for c in range(parts):
        after = cols * ((c + 1) % parts)
        before = cols * ((c - 1) % parts) + cols - EDGE
        for k in range(2):
            piece_ref[c, k, :, :cols] = disp_ref[k, :, cols * c:cols * (c + 1)]
            piece_ref[c, k, :, cols:] = jnp.where(
                lane < EDGE // 2, disp_ref[k, :, after:after + EDGE], disp_ref[k, :, before:before + EDGE]
            )


def rim(top_ref, bot_ref, left_ref, right_ref, dfirst_ref, dlast_ref, up_ref, down_ref):
    cols = top_ref.shape[2]
    last = bot_ref.shape[1] - 8
    rows = left_ref.shape[0]
    for k in range(5):
        up_ref[k, :, :cols] = top_ref[k, :8]
        up_ref[k, :, cols:] = unpack_edges(left_ref[:8], right_ref[:8], k)
        down_ref[k, :, :cols] = bot_ref[k, last:]
        down_ref[k, :, cols:] = unpack_edges(left_ref[rows - 8:], right_ref[rows - 8:], k)
    for k in range(4):
        up_ref[7, k:k + 1, :cols] = top_ref[k, 8:9]
        up_ref[7, k:k + 1, cols:] = unpack_edges(left_ref[8:16], right_ref[8:16], k)[:1]
        down_ref[7, k:k + 1, :cols] = bot_ref[k, last - 1:last]
        down_ref[7, k:k + 1, cols:] = unpack_edges(left_ref[rows - 16:rows - 8], right_ref[rows - 16:rows - 8], k)[7:]
    for k in range(2):
        up_ref[5 + k] = dfirst_ref[0, k]
        down_ref[5 + k] = dlast_ref[0, k]


def shift(x, axis, step):
    count = lax.axis_size(axis)
    return lax.ppermute(x, axis, [(i, (i + step) % count) for i in range(count)])


def on_device(conserved, displacement):
    rows, cols = conserved.shape[1:]
    parts = lax.axis_size("col")
    slab = displacement.shape[1]
    f32 = jnp.float32
    whole = pl.BlockSpec(memory_space=pltpu.VMEM)
    at = lambda shape, *index: pl.BlockSpec(shape, lambda i: index)
    first, last, pieces = pl.pallas_call(
        pack,
        out_shape=(
            jax.ShapeDtypeStruct((rows, EDGE), f32),
            jax.ShapeDtypeStruct((rows, EDGE), f32),
            jax.ShapeDtypeStruct((parts, 2, slab, cols + EDGE), f32),
        ),
        grid=(1,),
        in_specs=[
            at((5, rows, EDGE), 0, 0, 0),
            at((5, rows, EDGE), 0, 0, cols // EDGE - 1),
            at(displacement.shape, 0, 0, 0),
        ],
        out_specs=(
            at((rows, EDGE), 0, 0),
            at((rows, EDGE), 0, 0),
            at((parts, 2, slab, cols + EDGE), 0, 0, 0, 0),
        ),
        name="pack",
    )(conserved, conserved, displacement)
    dblk = lax.all_to_all(pieces, "col", 0, 0, tiled=True)
    left = shift(last, "col", 1)
    right = shift(first, "col", -1)
    payload = jax.ShapeDtypeStruct((8, 8, cols + EDGE), f32)
    up, down = pl.pallas_call(
        rim,
        out_shape=(payload, payload),
        grid=(1,),
        in_specs=[
            at((5, 16, cols), 0, 0, 0),
            at((5, 16, cols), 0, rows // 16 - 1, 0),
            at((rows, EDGE), 0, 0),
            at((rows, EDGE), 0, 0),
            at((1, 2, slab, cols + EDGE), 0, 0, 0, 0),
            at((1, 2, slab, cols + EDGE), parts - 1, 0, 0, 0),
        ],
        out_specs=(at(payload.shape, 0, 0, 0), at(payload.shape, 0, 0, 0)),
        name="rim",
    )(conserved, conserved, left, right, dblk, dblk)
    top = shift(down, "row", 1)
    bot = shift(up, "row", -1)
    return compute(conserved, left, right, dblk, top, bot)


def solution(mesh):
    placed = (P(None, "row", "col"), P(None, ("row", "col"), None))
    return jax.shard_map(
        on_device,
        mesh=mesh,
        in_specs=placed,
        out_specs=P("grp", None, "row", "col"),
        check_vma=False,
    )
```

time: 57.1 us -> 49.5 us (0.87)
  starting transfers between devices: 20.6 us -> 17.8 us
  waiting for transfers between devices: 10.3 us -> 8.32 us
  Pallas kernels: 21.8 us -> 20.3 us
  other arithmetic: 0.82 us -> 0 us
    ppermute x6 -> x4, starting transfers between devices: 15.9 us -> 9.85 us  [shift(): lax.ppermute(x, axis, [(i, (i + step) % count) for i in range(count)])]
    pallas_call x1, Pallas kernels: 21.8 us -> 16.5 us  [compute(): pl.pallas_call(core, out_shape=jax.ShapeDtypeStruct((1, 5, rows, cols), j...]
    all_to_all x1, waiting for transfers between devices: 4.1 us -> 0.01 us  [on_device(): dblk = lax.all_to_all(pieces, 'col', 0, 0, tiled=True)]
    pallas_call x0 -> x2, Pallas kernels: none -> 3.8 us  [the longest x1 1.99 us: on_device(): pl.pallas_call(pack, out_shape=(jax.ShapeDtypeStruct((rows, EDGE), f32),...]
    all_to_all x1, starting transfers between devices: 4.72 us -> 7.99 us  [on_device(): dblk = lax.all_to_all(pieces, 'col', 0, 0, tiled=True)]
    ppermute x6 -> x4, waiting for transfers between devices: 6.19 us -> 8.31 us  [shift(): lax.ppermute(x, axis, [(i, (i + step) % count) for i in range(count)])]
    slice x5 -> x0, local copies, waits for them, and re-layouts: 1.14 us -> none  [the longest x1 1.06 us: on_device(): from_left = shift(conserved[:, :, cols - EDGE:], 'col', 1)]
    concatenate x3 -> x0, other arithmetic: 0.78 us -> none  [the longest x1 0.75 us: on_device(): jnp.concatenate([pieces, jnp.where(lane < EDGE // 2, right, left)], -1)]
  transfers between devices with their start and end apart: 7 -> 5, of which waited for: 4 -> 2; matrix products, arithmetic and copies ran while one was open for 2% -> 0% of each run, Pallas kernels for 0% -> 0%
where the time goes in v2:
time: 49.5 us; the launch traced here: 49.2 us
  Pallas kernels  20.3 us (41%)
  starting transfers between devices  17.8 us (36%)
  waiting for transfers between devices  8.32 us (17%)
  local copies, waits for them, and re-layouts  2.66 us (5%)
    pallas_call x1, Pallas kernels, compute(): pl.pallas_call(core, out_shape=jax.ShapeDtypeStruct((1, 5, rows, cols), j...  16.5 us
    ppermute x4, starting transfers between devices, shift(): lax.ppermute(x, axis, [(i, (i + step) % count) for i in range(count)])  9.85 us
    ppermute x4, waiting for transfers between devices, shift(): lax.ppermute(x, axis, [(i, (i + step) % count) for i in range(count)])  8.31 us
    all_to_all x1, starting transfers between devices, on_device(): dblk = lax.all_to_all(pieces, 'col', 0, 0, tiled=True)  7.99 us
    unnamed x14, local copies, waits for them, and re-layouts  2.66 us
    pallas_call x1, Pallas kernels, on_device(): pl.pallas_call(pack, out_shape=(jax.ShapeDtypeStruct((rows, EDGE), f32),...  1.99 us
    pallas_call x1, Pallas kernels, on_device(): pl.pallas_call(rim, out_shape=(payload, payload), grid=(1,), in_specs=[at...  1.82 us
  transfers between devices with their start and end apart: 5, of which 2 were waited for; matrix products, arithmetic and copies ran while one was open for 0% of the time, Pallas kernels for 0%

profile of v2, /device:TPU:0, one launch (start us, length us, event | category | flops | bytes accessed | tf_op | source)
XLA Modules:
  0.0 49.2 jit_solution(4016105545343476538)
XLA Ops:
  0.0 2.0 %pack.1 = (f32[64,128]{1,0:T(8,128)}, f32[64,128]{1,0:T(8,128)}, f32[8,2,8,640]{3,2,1,0:T(8,128)}) custom-call(f32[5,64,512]{2,1,0:T(8,128)} %u_ref.1, f32[5,64,512]{2,1,0:T(8,128)} %u_ref.1, f32[2,8,4096]{2,1,0:T(8,128)} %disp_ref.1), custom_call_target="tpu_custom_call" | custom-call | tf_op jit(solution)/shard_map/pack/pallas_call | solution.py:371
  2.0 0.0 copy-start.6
  2.0 0.0 copy-start.5
  2.0 8.0 %all-to-all-start = ((f32[8,2,8,640]{3,2,1,0:T(8,128)}), f32[8,2,8,640]{3,2,1,0:T(8,128)S(1)}, u32[]{:S(2)}, u32[]{:S(2)}) async-start(f32[8,2,8,640]{3,2,1,0:T(8,128)} %get-tuple-element.12), calls=%async_computation | async-start | bytes 655360 | tf_op jit(solution)/shard_map/all_to_all | solution.py:391
  10.0 0.0 copy-done.6
  10.0 3.5 %collective-permute-start = (f32[64,128]{1,0:T(8,128)S(1)}, f32[64,128]{1,0:T(8,128)S(1)}, u32[]{:S(2)}, u32[]{:S(2)}) collective-permute-start(f32[64,128]{1,0:T(8,128)S(1)} %copy-done.6), channel_id=1, source_target_pairs={{0,1},{1,2},{2,3},{3,4},{4,5},{5,6},{6,7},{7,0},{8,9},{9,10},{10,1... | collective-permute-start | bytes 98312 | tf_op jit(solution)/shard_map/ppermute | solution.py:361
  13.5 0.0 copy-done.5
  13.5 2.2 %collective-permute-start.1 = (f32[64,128]{1,0:T(8,128)S(1)}, f32[64,128]{1,0:T(8,128)S(1)}, u32[]{:S(2)}, u32[]{:S(2)}) collective-permute-start(f32[64,128]{1,0:T(8,128)S(1)} %copy-done.5), channel_id=1, source_target_pairs={{0,7},{1,0},{2,1},{3,2},{4,3},{5,4},{6,5},{7,6},{8,15},{9,8},{10,9... | collective-permute-start | bytes 98312 | tf_op jit(solution)/shard_map/ppermute | solution.py:361
  15.7 4.8 %collective-permute-done.left_ref = f32[64,128]{1,0:T(8,128)S(1)} collective-permute-done((f32[64,128]{1,0:T(8,128)S(1)}, f32[64,128]{1,0:T(8,128)S(1)}, u32[]{:S(2)}, u32[]{:S(2)}) %collective-permute-start) | collective-permute-done | bytes 32800 | tf_op jit(solution)/shard_map/ppermute | solution.py:361
  20.5 0.0 copy-start.3
  20.5 0.0 collective-permute-done.1.right_ref
  20.5 0.0 copy-start.4
  20.5 0.0 all-to-all-done.dfirst_ref.dlast_ref.dblk_ref
  20.5 0.6 %copy-done.3 = f32[64,128]{1,0:T(8,128)} copy-done((f32[64,128]{1,0:T(8,128)}, f32[64,128]{1,0:T(8,128)S(1)}, u32[]{:S(2)}) %copy-start.3) | copy-done | bytes 32792
  21.1 0.0 copy-done.4
  21.1 0.0 copy-start
  21.1 0.7 %copy-done = f32[8,2,8,640]{3,2,1,0:T(8,128)} copy-done((f32[8,2,8,640]{3,2,1,0:T(8,128)}, f32[8,2,8,640]{3,2,1,0:T(8,128)S(1)}, u32[]{:S(2)}) %copy-start) | copy-done | bytes 327704
  21.9 1.8 %rim.1 = (f32[8,8,640]{2,1,0:T(8,128)}, f32[8,8,640]{2,1,0:T(8,128)}) custom-call(f32[5,64,512]{2,1,0:T(8,128)} %u_ref.1, f32[5,64,512]{2,1,0:T(8,128)} %u_ref.1, f32[64,128]{1,0:T(8,128)} %copy-done.3, f32[64,128]{1,0:T(8,128)} %copy-done.4, f32[8,2,8,640]{3,2,1,0:T(8,128)} %copy-done, f32[8,2,8,640]{3,2,1,0:T(8,128)} %copy-done), custom_call_target="tpu_custom_call" | custom-call | tf_op jit(solution)/shard_map/rim/pallas_call | solution.py:395
  23.7 1.6 %collective-permute-start.2 = (f32[8,8,640]{2,1,0:T(8,128)}, f32[8,8,640]{2,1,0:T(8,128)S(1)}, u32[]{:S(2)}, u32[]{:S(2)}) collective-permute-start(f32[8,8,640]{2,1,0:T(8,128)} %get-tuple-element.13), channel_id=1, source_target_pairs={{0,8},{8,16},{16,24},{24,32},{32,40},{40,48},{48,56},{56,0},{1,9},... | collective-permute-start | bytes 491528 | tf_op jit(solution)/shard_map/ppermute | solution.py:361
  25.3 2.6 %collective-permute-start.3 = (f32[8,8,640]{2,1,0:T(8,128)}, f32[8,8,640]{2,1,0:T(8,128)S(1)}, u32[]{:S(2)}, u32[]{:S(2)}) collective-permute-start(f32[8,8,640]{2,1,0:T(8,128)} %get-tuple-element.14), channel_id=1, source_target_pairs={{0,56},{8,0},{16,8},{24,16},{32,24},{40,32},{48,40},{56,48},{1,57}... | collective-permute-start | bytes 491528 | tf_op jit(solution)/shard_map/ppermute | solution.py:361
  27.8 3.5 %collective-permute-done.2.top_ref = f32[8,8,640]{2,1,0:T(8,128)S(1)} collective-permute-done((f32[8,8,640]{2,1,0:T(8,128)}, f32[8,8,640]{2,1,0:T(8,128)S(1)}, u32[]{:S(2)}, u32[]{:S(2)}) %collective-permute-start.2) | collective-permute-done | bytes 163872 | tf_op jit(solution)/shard_map/ppermute | solution.py:361
  31.3 0.0 copy-start.1
  31.3 0.0 collective-permute-done.3.bot_ref
  31.3 0.7 %copy-done.1 = f32[8,8,640]{2,1,0:T(8,128)} copy-done((f32[8,8,640]{2,1,0:T(8,128)}, f32[8,8,640]{2,1,0:T(8,128)S(1)}, u32[]{:S(2)}) %copy-start.1) | copy-done | bytes 163864
  32.0 0.0 copy-start.2
  32.0 0.7 %copy-done.2 = f32[8,8,640]{2,1,0:T(8,128)} copy-done((f32[8,8,640]{2,1,0:T(8,128)}, f32[8,8,640]{2,1,0:T(8,128)S(1)}, u32[]{:S(2)}) %copy-start.2) | copy-done | bytes 163864
  32.6 16.5 %euler_mesh.1 = f32[1,5,64,512]{3,2,1,0:T(8,128)} custom-call(f32[5,64,512]{2,1,0:T(8,128)} %u_ref.1, f32[64,128]{1,0:T(8,128)} %copy-done.3, f32[64,128]{1,0:T(8,128)} %copy-done.4, f32[8,2,8,640]{3,2,1,0:T(8,128)} %copy-done, f32[8,8,640]{2,1,0:T(8,128)} %copy-done.1, f32[8,8,640]{2,1,0:T(8,128)} %copy-done.2), custom_call_target="tpu_custom_call" | custom-call | tf_op jit(solution)/shard_map/euler_mesh/pallas_call | solution.py:301
Async XLA Ops:
  2.0 8.0 %copy-start.6 = (f32[64,128]{1,0:T(8,128)S(1)}, f32[64,128]{1,0:T(8,128)}, u32[]{:S(2)}) copy-start(f32[64,128]{1,0:T(8,128)} %get-tuple-element.10) | copy-start | bytes 98308
  2.0 11.5 %copy-start.5 = (f32[64,128]{1,0:T(8,128)S(1)}, f32[64,128]{1,0:T(8,128)}, u32[]{:S(2)}) copy-start(f32[64,128]{1,0:T(8,128)} %get-tuple-element.11) | copy-start | bytes 98308
  2.0 18.5 %all-to-all-start = ((f32[8,2,8,640]{3,2,1,0:T(8,128)}), f32[8,2,8,640]{3,2,1,0:T(8,128)S(1)}, u32[]{:S(2)}, u32[]{:S(2)}) async-start(f32[8,2,8,640]{3,2,1,0:T(8,128)} %get-tuple-element.12), calls=%async_computation | async-start | bytes 655360 | tf_op jit(solution)/shard_map/all_to_all | solution.py:391
  10.0 10.5 %collective-permute-start = (f32[64,128]{1,0:T(8,128)S(1)}, f32[64,128]{1,0:T(8,128)S(1)}, u32[]{:S(2)}, u32[]{:S(2)}) collective-permute-start(f32[64,128]{1,0:T(8,128)S(1)} %copy-done.6), channel_id=1, source_target_pairs={{0,1},{1,2},{2,3},{3,4},{4,5},{5,6},{6,7},{7,0},{8,9},{9,10},{10,1... | collective-permute-start | bytes 98312 | tf_op jit(solution)/shard_map/ppermute | solution.py:361
  13.5 7.0 %collective-permute-start.1 = (f32[64,128]{1,0:T(8,128)S(1)}, f32[64,128]{1,0:T(8,128)S(1)}, u32[]{:S(2)}, u32[]{:S(2)}) collective-permute-start(f32[64,128]{1,0:T(8,128)S(1)} %copy-done.5), channel_id=1, source_target_pairs={{0,7},{1,0},{2,1},{3,2},{4,3},{5,4},{6,5},{7,6},{8,15},{9,8},{10,9... | collective-permute-start | bytes 98312 | tf_op jit(solution)/shard_map/ppermute | solution.py:361
  20.5 0.6 %copy-start.3 = (f32[64,128]{1,0:T(8,128)}, f32[64,128]{1,0:T(8,128)S(1)}, u32[]{:S(2)}) copy-start(f32[64,128]{1,0:T(8,128)S(1)} %collective-permute-done.left_ref) | copy-start | bytes 98308
  20.5 0.6 %copy-start.4 = (f32[64,128]{1,0:T(8,128)}, f32[64,128]{1,0:T(8,128)S(1)}, u32[]{:S(2)}) copy-start(f32[64,128]{1,0:T(8,128)S(1)} %collective-permute-done.1.right_ref) | copy-start | bytes 98308
  21.1 0.7 %copy-start = (f32[8,2,8,640]{3,2,1,0:T(8,128)}, f32[8,2,8,640]{3,2,1,0:T(8,128)S(1)}, u32[]{:S(2)}) copy-start(f32[8,2,8,640]{3,2,1,0:T(8,128)S(1)} %all-to-all-done.dfirst_ref.dlast_ref.dblk_ref) | copy-start | bytes 983044
  23.7 7.6 %collective-permute-start.2 = (f32[8,8,640]{2,1,0:T(8,128)}, f32[8,8,640]{2,1,0:T(8,128)S(1)}, u32[]{:S(2)}, u32[]{:S(2)}) collective-permute-start(f32[8,8,640]{2,1,0:T(8,128)} %get-tuple-element.13), channel_id=1, source_target_pairs={{0,8},{8,16},{16,24},{24,32},{32,40},{40,48},{48,56},{56,0},{1,9},... | collective-permute-start | bytes 491528 | tf_op jit(solution)/shard_map/ppermute | solution.py:361
  25.3 6.1 %collective-permute-start.3 = (f32[8,8,640]{2,1,0:T(8,128)}, f32[8,8,640]{2,1,0:T(8,128)S(1)}, u32[]{:S(2)}, u32[]{:S(2)}) collective-permute-start(f32[8,8,640]{2,1,0:T(8,128)} %get-tuple-element.14), channel_id=1, source_target_pairs={{0,56},{8,0},{16,8},{24,16},{32,24},{40,32},{48,40},{56,48},{1,57}... | collective-permute-start | bytes 491528 | tf_op jit(solution)/shard_map/ppermute | solution.py:361
  31.3 0.7 %copy-start.1 = (f32[8,8,640]{2,1,0:T(8,128)}, f32[8,8,640]{2,1,0:T(8,128)S(1)}, u32[]{:S(2)}) copy-start(f32[8,8,640]{2,1,0:T(8,128)S(1)} %collective-permute-done.2.top_ref) | copy-start | bytes 491524
  32.0 0.7 %copy-start.2 = (f32[8,8,640]{2,1,0:T(8,128)}, f32[8,8,640]{2,1,0:T(8,128)S(1)}, u32[]{:S(2)}) copy-start(f32[8,8,640]{2,1,0:T(8,128)S(1)} %collective-permute-done.3.bot_ref) | copy-start | bytes 491524

commit v3 on v2

--- a/solution.py
+++ b/solution.py
@@ -15,7 +15,9 @@
 EXT = 8 * BAND
 PAD = 8
 EDGE = 128
-SLOT = 16
+SLOT = 12
+HALF = 32
+DTILES = 10
 
 
 def next_col(x):
@@ -194,14 +196,20 @@
     return face[2, t] * ((c - prev_col(c)) + (rowfl[k, t + 1] - rowfl[k, t]))
 
 
-def unpack_edges(left, right, k):
+def unpack_edges(left, right, k, half):
     lane = lax.broadcasted_iota(jnp.int32, left.shape, 1)
-    a = pltpu.roll(right, (EDGE - SLOT * k) % EDGE, 1)
-    b = pltpu.roll(left, (EDGE - SLOT - SLOT * k) % EDGE, 1)
+    start = EDGE // 2 * half + SLOT * k
+    a = pltpu.roll(right, (EDGE - start) % EDGE, 1)
+    b = pltpu.roll(left, (EDGE - SLOT - start) % EDGE, 1)
     return jnp.where(lane < EDGE // 2, a, b)
 
 
-def core(u_ref, left_ref, right_ref, dblk_ref, top_ref, bot_ref, out_ref,
+def beside(parts):
+    c = lax.axis_index("col")
+    return lax.rem(c + parts - 1, parts), lax.rem(c + 1, parts)
+
+
+def core(u_ref, piece_ref, top_ref, bot_ref, out_ref,
          ext, prim, half, side, face, slope, colfl, rowfl, weight, coef, da, db, cons, flat):
     rows, cols = u_ref.shape[1], u_ref.shape[2]
     tiles = cols // EDGE + 1
@@ -210,13 +218,18 @@
         for j in range(value.shape[1] // EDGE):
             ext[k, j, row:row + value.shape[0], :] = value[:, EDGE * j:EDGE * (j + 1)]
 
-    left, right = left_ref[...], right_ref[...]
+    before, after = beside(piece_ref.shape[0])
     for k in range(5):
         place(k, PAD, u_ref[k])
-        ext[k, tiles - 1, PAD:PAD + rows, :] = unpack_edges(left, right, k)
+        for g in range(HALF // 8):
+            left, right = piece_ref[before, DTILES + g], piece_ref[after, DTILES + g]
+            for h in range(2):
+                row = PAD + HALF * h + 8 * g
+                ext[k, tiles - 1, row:row + 8, :] = unpack_edges(left, right, k, h)
     for k in range(2):
-        for c in range(dblk_ref.shape[0]):
-            place(5 + k, PAD + 8 * c, dblk_ref[c, k])
+        for c in range(piece_ref.shape[0]):
+            for j in range(tiles):
+                ext[5 + k, j, PAD + 8 * c:PAD + 8 * c + 8, :] = piece_ref[c, tiles * k + j]
     for k in range(7):
         place(k, 0, top_ref[k])
         place(k, PAD + rows, bot_ref[k])
@@ -294,14 +307,18 @@
 U_FLUX = 1
 
 
-def compute(u, left, right, dblk, top, bot):
+def near(x):
+    return pltpu.with_memory_space_constraint(x, pltpu.VMEM)
+
+
+def compute(u, pieces, top, bot):
     rows, cols = u.shape[1], u.shape[2]
     wide = cols + EDGE
     vec = lambda *lead: pltpu.VMEM((*lead, 8, wide), jnp.float32)
     return pl.pallas_call(
         core,
         out_shape=jax.ShapeDtypeStruct((1, 5, rows, cols), jnp.float32),
-        in_specs=[pl.BlockSpec(memory_space=pltpu.VMEM)] * 6,
+        in_specs=[pl.BlockSpec(memory_space=pltpu.VMEM)] * 4,
         out_specs=pl.BlockSpec(memory_space=pltpu.VMEM),
         scratch_shapes=[
             pltpu.VMEM((7, wide // EDGE, EXT, EDGE), jnp.float32),
@@ -311,49 +328,64 @@
             pltpu.VMEM((5, cols // EDGE, EXT, EDGE), jnp.float32),
         ],
         name="euler_mesh",
-    )(u, left, right, dblk, top, bot)
-
-
-def pack(first_ref, last_ref, disp_ref, left_ref, right_ref, piece_ref):
-    lane = lax.broadcasted_iota(jnp.int32, left_ref.shape, 1)
-    left = right = None
-    for k in range(5):
-        a = pltpu.roll(first_ref[k], SLOT * k, 1) if k else first_ref[k]
-        b = pltpu.roll(last_ref[k], (SLOT + SLOT * k) % EDGE, 1)
-        left = a if left is None else jnp.where(lane < SLOT * k, left, a)
-        right = b if right is None else jnp.where(lane < SLOT * k, right, b)
-    left_ref[...] = left
-    right_ref[...] = right
+    )(u, near(pieces), near(top), near(bot))
+
+
+def pack(first_ref, last_ref, disp_ref, piece_ref):
     parts = piece_ref.shape[0]
-    cols = piece_ref.shape[3] - EDGE
-    lane = lax.broadcasted_iota(jnp.int32, (disp_ref.shape[1], EDGE), 1)
+    tiles = DTILES // 2
+    cols = EDGE * (tiles - 1)
+    before, after = beside(parts)
+    lane = lax.broadcasted_iota(jnp.int32, (8, EDGE), 1)
+    for g in range(HALF // 8):
+        first = last = None
+        for half in range(2):
+            rows = slice(HALF * half + 8 * g, HALF * half + 8 * g + 8)
+            for k in range(5):
+                start = EDGE // 2 * half + SLOT * k
+                a = pltpu.roll(first_ref[k, rows], start, 1) if start else first_ref[k, rows]
+                b = pltpu.roll(last_ref[k, rows], SLOT + start, 1)
+                first = a if first is None else jnp.where(lane < start, first, a)
+                last = b if last is None else jnp.where(lane < start, last, b)
+        piece_ref[before, DTILES + g] = first
+        piece_ref[after, DTILES + g] = last
     for c in range(parts):
-        after = cols * ((c + 1) % parts)
-        before = cols * ((c - 1) % parts) + cols - EDGE
+        right = cols * ((c + 1) % parts)
+        left = cols * ((c - 1) % parts) + cols - EDGE
         for k in range(2):
-            piece_ref[c, k, :, :cols] = disp_ref[k, :, cols * c:cols * (c + 1)]
-            piece_ref[c, k, :, cols:] = jnp.where(
-                lane < EDGE // 2, disp_ref[k, :, after:after + EDGE], disp_ref[k, :, before:before + EDGE]
+            for j in range(tiles - 1):
+                at = cols * c + EDGE * j
+                piece_ref[c, tiles * k + j] = disp_ref[k, :, at:at + EDGE]
+            piece_ref[c, tiles * k + tiles - 1] = jnp.where(
+                lane < EDGE // 2, disp_ref[k, :, right:right + EDGE], disp_ref[k, :, left:left + EDGE]
             )
 
 
-def rim(top_ref, bot_ref, left_ref, right_ref, dfirst_ref, dlast_ref, up_ref, down_ref):
+def rim(top_ref, bot_ref, piece_ref, up_ref, down_ref):
     cols = top_ref.shape[2]
-    last = bot_ref.shape[1] - 8
-    rows = left_ref.shape[0]
+    tiles = cols // EDGE + 1
+    end = bot_ref.shape[1] - 8
+    parts = piece_ref.shape[0]
+    before, after = beside(parts)
+    final = DTILES + HALF // 8 - 1
+    l0, r0 = piece_ref[before, DTILES], piece_ref[after, DTILES]
+    l1, r1 = piece_ref[before, final], piece_ref[after, final]
     for k in range(5):
         up_ref[k, :, :cols] = top_ref[k, :8]
-        up_ref[k, :, cols:] = unpack_edges(left_ref[:8], right_ref[:8], k)
-        down_ref[k, :, :cols] = bot_ref[k, last:]
-        down_ref[k, :, cols:] = unpack_edges(left_ref[rows - 8:], right_ref[rows - 8:], k)
+        up_ref[k, :, cols:] = unpack_edges(l0, r0, k, 0)
+        down_ref[k, :, :cols] = bot_ref[k, end:]
+        down_ref[k, :, cols:] = unpack_edges(l1, r1, k, 1)
+    l0, r0 = piece_ref[before, DTILES + 1], piece_ref[after, DTILES + 1]
+    l1, r1 = piece_ref[before, final - 1], piece_ref[after, final - 1]
     for k in range(4):
         up_ref[7, k:k + 1, :cols] = top_ref[k, 8:9]
-        up_ref[7, k:k + 1, cols:] = unpack_edges(left_ref[8:16], right_ref[8:16], k)[:1]
-        down_ref[7, k:k + 1, :cols] = bot_ref[k, last - 1:last]
-        down_ref[7, k:k + 1, cols:] = unpack_edges(left_ref[rows - 16:rows - 8], right_ref[rows - 16:rows - 8], k)[7:]
+        up_ref[7, k:k + 1, cols:] = unpack_edges(l0, r0, k, 0)[:1]
+        down_ref[7, k:k + 1, :cols] = bot_ref[k, end - 1:end]
+        down_ref[7, k:k + 1, cols:] = unpack_edges(l1, r1, k, 1)[7:]
     for k in range(2):
-        up_ref[5 + k] = dfirst_ref[0, k]
-        down_ref[5 + k] = dlast_ref[0, k]
+        for j in range(tiles):
+            up_ref[5 + k, :, EDGE * j:EDGE * (j + 1)] = piece_ref[0, tiles * k + j]
+            down_ref[5 + k, :, EDGE * j:EDGE * (j + 1)] = piece_ref[parts - 1, tiles * k + j]
 
 
 def shift(x, axis, step):
@@ -364,34 +396,23 @@
 def on_device(conserved, displacement):
     rows, cols = conserved.shape[1:]
     parts = lax.axis_size("col")
-    slab = displacement.shape[1]
     f32 = jnp.float32
+    at = lambda shape, *index: pl.BlockSpec(shape, lambda i: index)
     whole = pl.BlockSpec(memory_space=pltpu.VMEM)
-    at = lambda shape, *index: pl.BlockSpec(shape, lambda i: index)
-    first, last, pieces = pl.pallas_call(
+    pieces = pl.pallas_call(
         pack,
-        out_shape=(
-            jax.ShapeDtypeStruct((rows, EDGE), f32),
-            jax.ShapeDtypeStruct((rows, EDGE), f32),
-            jax.ShapeDtypeStruct((parts, 2, slab, cols + EDGE), f32),
-        ),
+        out_shape=pltpu.VMEM((parts, DTILES + HALF // 8, 8, EDGE), f32),
         grid=(1,),
         in_specs=[
             at((5, rows, EDGE), 0, 0, 0),
             at((5, rows, EDGE), 0, 0, cols // EDGE - 1),
             at(displacement.shape, 0, 0, 0),
         ],
-        out_specs=(
-            at((rows, EDGE), 0, 0),
-            at((rows, EDGE), 0, 0),
-            at((parts, 2, slab, cols + EDGE), 0, 0, 0, 0),
-        ),
+        out_specs=whole,
         name="pack",
     )(conserved, conserved, displacement)
-    dblk = lax.all_to_all(pieces, "col", 0, 0, tiled=True)
-    left = shift(last, "col", 1)
-    right = shift(first, "col", -1)
-    payload = jax.ShapeDtypeStruct((8, 8, cols + EDGE), f32)
+    pieces = lax.all_to_all(pieces, "col", 0, 0, tiled=True)
+    payload = pltpu.VMEM((8, 8, cols + EDGE), f32)
     up, down = pl.pallas_call(
         rim,
         out_shape=(payload, payload),
@@ -399,17 +420,14 @@
         in_specs=[
             at((5, 16, cols), 0, 0, 0),
             at((5, 16, cols), 0, rows // 16 - 1, 0),
-            at((rows, EDGE), 0, 0),
-            at((rows, EDGE), 0, 0),
-            at((1, 2, slab, cols + EDGE), 0, 0, 0, 0),
-            at((1, 2, slab, cols + EDGE), parts - 1, 0, 0, 0),
+            whole,
         ],
-        out_specs=(at(payload.shape, 0, 0, 0), at(payload.shape, 0, 0, 0)),
+        out_specs=(whole, whole),
         name="rim",
-    )(conserved, conserved, left, right, dblk, dblk)
+    )(conserved, conserved, near(pieces))
     top = shift(down, "row", 1)
     bot = shift(up, "row", -1)
-    return compute(conserved, left, right, dblk, top, bot)
+    return compute(conserved, pieces, top, bot)
 
 
 def solution(mesh):

time: 49.5 us -> 45.2 us (0.913)
  blocking collectives: 0 us -> 18.6 us
  starting transfers between devices: 17.8 us -> 4.2 us
  waiting for transfers between devices: 8.32 us -> 3.29 us
  local copies, waits for them, and re-layouts: 2.66 us -> 0 us
  Pallas kernels: 20.3 us -> 18.7 us
    all_to_all x0 -> x1, blocking collectives: none -> 18.6 us  [on_device(): pieces = lax.all_to_all(pieces, 'col', 0, 0, tiled=True)]
    all_to_all x1 -> x0, starting transfers between devices: 7.99 us -> none  [on_device(): dblk = lax.all_to_all(pieces, 'col', 0, 0, tiled=True)]
    ppermute x4 -> x2, starting transfers between devices: 9.85 us -> 4.2 us  [shift(): lax.ppermute(x, axis, [(i, (i + step) % count) for i in range(count)])]
    ppermute x4 -> x2, waiting for transfers between devices: 8.31 us -> 3.29 us  [shift(): lax.ppermute(x, axis, [(i, (i + step) % count) for i in range(count)])]
    unnamed x14 -> x0, local copies, waits for them, and re-layouts: 2.66 us -> none
    pallas_call x1, Pallas kernels: 1.82 us -> 1.11 us  [on_device(): pl.pallas_call(rim, out_shape=(payload, payload), grid=(1,), in_specs=[at...]
    pallas_call x1, Pallas kernels: 1.99 us -> 1.29 us  [on_device(): pl.pallas_call(pack, out_shape=pltpu.VMEM((parts, DTILES + HALF // 8, 8,...]
  transfers between devices with their start and end apart: 5 -> 2, of which waited for: 2 -> 1; matrix products, arithmetic and copies ran while one was open for 0% -> 0% of each run, Pallas kernels for 0% -> 0%
where the time goes in v3:
time: 45.2 us; the launch traced here: 44.8 us
  Pallas kernels  18.7 us (41%)
  blocking collectives  18.6 us (41%)
  starting transfers between devices  4.2 us (9%)
  waiting for transfers between devices  3.29 us (7%)
    all_to_all x1, blocking collectives, on_device(): pieces = lax.all_to_all(pieces, 'col', 0, 0, tiled=True)  18.6 us
    pallas_call x1, Pallas kernels, compute(): pl.pallas_call(core, out_shape=jax.ShapeDtypeStruct((1, 5, rows, cols), j...  16.3 us
    ppermute x2, starting transfers between devices, shift(): lax.ppermute(x, axis, [(i, (i + step) % count) for i in range(count)])  4.2 us
    ppermute x2, waiting for transfers between devices, shift(): lax.ppermute(x, axis, [(i, (i + step) % count) for i in range(count)])  3.29 us
    pallas_call x1, Pallas kernels, on_device(): pl.pallas_call(pack, out_shape=pltpu.VMEM((parts, DTILES + HALF // 8, 8,...  1.29 us
    pallas_call x1, Pallas kernels, on_device(): pl.pallas_call(rim, out_shape=(payload, payload), grid=(1,), in_specs=[at...  1.11 us
  transfers between devices with their start and end apart: 2, of which 1 were waited for; matrix products, arithmetic and copies ran while one was open for 0% of the time, Pallas kernels for 0%

profile of v3, /device:TPU:0, one launch (start us, length us, event | category | flops | bytes accessed | tf_op | source)
XLA Modules:
  0.0 44.8 jit_solution(15382419424939983653)
XLA Ops:
  0.0 1.3 %pack.1 = f32[8,14,8,128]{3,2,1,0:T(8,128)S(1)} custom-call(f32[5,64,512]{2,1,0:T(8,128)} %u_ref.1, f32[5,64,512]{2,1,0:T(8,128)} %u_ref.1, f32[2,8,4096]{2,1,0:T(8,128)} %disp_ref.1), custom_call_target="tpu_custom_call" | custom-call | tf_op jit(solution)/shard_map/pack/pallas_call | solution.py:402
  1.3 18.6 %all_to_all.5.piece_ref = f32[8,14,8,128]{3,2,1,0:T(8,128)S(1)} all-to-all(f32[8,14,8,128]{3,2,1,0:T(8,128)S(1)} %pack.1), channel_id=1, replica_groups=mesh['grp'=2,'row'=8,'col'=8] {'col'}, dimensions={0} | all-to-all | bytes 917504 | tf_op jit(solution)/shard_map/all_to_all | solution.py:414
  19.9 1.1 %rim.1 = (f32[8,8,640]{2,1,0:T(8,128)S(1)}, f32[8,8,640]{2,1,0:T(8,128)S(1)}) custom-call(f32[5,64,512]{2,1,0:T(8,128)} %u_ref.1, f32[5,64,512]{2,1,0:T(8,128)} %u_ref.1, f32[8,14,8,128]{3,2,1,0:T(8,128)S(1)} %all_to_all.5.piece_ref), custom_call_target="tpu_custom_call" | custom-call | tf_op jit(solution)/shard_map/rim/pallas_call | solution.py:416
  21.0 1.6 %collective-permute-start = (f32[8,8,640]{2,1,0:T(8,128)S(1)}, f32[8,8,640]{2,1,0:T(8,128)S(1)}, u32[]{:S(2)}, u32[]{:S(2)}) collective-permute-start(f32[8,8,640]{2,1,0:T(8,128)S(1)} %get-tuple-element.7), channel_id=1, source_target_pairs={{0,8},{8,16},{16,24},{24,32},{32,40},{40,48},{48,56},{56,0},{1,9},... | collective-permute-start | bytes 491528 | tf_op jit(solution)/shard_map/ppermute | solution.py:393
  22.6 2.6 %collective-permute-start.1 = (f32[8,8,640]{2,1,0:T(8,128)S(1)}, f32[8,8,640]{2,1,0:T(8,128)S(1)}, u32[]{:S(2)}, u32[]{:S(2)}) collective-permute-start(f32[8,8,640]{2,1,0:T(8,128)S(1)} %get-tuple-element.8), channel_id=1, source_target_pairs={{0,56},{8,0},{16,8},{24,16},{32,24},{40,32},{48,40},{56,48},{1,57}... | collective-permute-start | bytes 491528 | tf_op jit(solution)/shard_map/ppermute | solution.py:393
  25.2 3.3 %collective-permute-done.top_ref = f32[8,8,640]{2,1,0:T(8,128)S(1)} collective-permute-done((f32[8,8,640]{2,1,0:T(8,128)S(1)}, f32[8,8,640]{2,1,0:T(8,128)S(1)}, u32[]{:S(2)}, u32[]{:S(2)}) %collective-permute-start) | collective-permute-done | bytes 163872 | tf_op jit(solution)/shard_map/ppermute | solution.py:393
  28.5 0.0 collective-permute-done.1.bot_ref
  28.5 16.3 %euler_mesh.1 = f32[1,5,64,512]{3,2,1,0:T(8,128)} custom-call(f32[5,64,512]{2,1,0:T(8,128)} %u_ref.1, f32[8,14,8,128]{3,2,1,0:T(8,128)S(1)} %all_to_all.5.piece_ref, f32[8,8,640]{2,1,0:T(8,128)S(1)} %collective-permute-done.top_ref, f32[8,8,640]{2,1,0:T(8,128)S(1)} %collective-permute-done.1.bot_ref), custom_call_target="tpu_custom_call" | custom-call | tf_op jit(solution)/shard_map/euler_mesh/pallas_call | solution.py:318
Async XLA Ops:
  21.0 7.5 %collective-permute-start = (f32[8,8,640]{2,1,0:T(8,128)S(1)}, f32[8,8,640]{2,1,0:T(8,128)S(1)}, u32[]{:S(2)}, u32[]{:S(2)}) collective-permute-start(f32[8,8,640]{2,1,0:T(8,128)S(1)} %get-tuple-element.7), channel_id=1, source_target_pairs={{0,8},{8,16},{16,24},{24,32},{32,40},{40,48},{48,56},{56,0},{1,9},... | collective-permute-start | bytes 491528 | tf_op jit(solution)/shard_map/ppermute | solution.py:393
  22.6 5.9 %collective-permute-start.1 = (f32[8,8,640]{2,1,0:T(8,128)S(1)}, f32[8,8,640]{2,1,0:T(8,128)S(1)}, u32[]{:S(2)}, u32[]{:S(2)}) collective-permute-start(f32[8,8,640]{2,1,0:T(8,128)S(1)} %get-tuple-element.8), channel_id=1, source_target_pairs={{0,56},{8,0},{16,8},{24,16},{32,24},{40,32},{48,40},{56,48},{1,57}... | collective-permute-start | bytes 491528 | tf_op jit(solution)/shard_map/ppermute | solution.py:393

commit v4 on v3

--- a/solution.py
+++ b/solution.py
@@ -17,7 +17,7 @@
 EDGE = 128
 SLOT = 12
 HALF = 32
-DTILES = 10
+DTILES = 9
 
 
 def next_col(x):
@@ -204,6 +204,19 @@
     return jnp.where(lane < EDGE // 2, a, b)
 
 
+def join_halos(after, before):
+    lane = lax.broadcasted_iota(jnp.int32, after[0].shape, 1)
+    low = jnp.where(lane < 32, after[0], pltpu.roll(before[0], EDGE // 2, 1))
+    high = jnp.where(lane < 96, pltpu.roll(after[1], EDGE // 2, 1), before[1])
+    return jnp.where(lane < EDGE // 2, low, high)
+
+
+def split_halos(x):
+    lane = lax.broadcasted_iota(jnp.int32, x.shape, 1)
+    y = pltpu.roll(x, EDGE // 2, 1)
+    return jnp.where(lane < EDGE // 2, x, y), jnp.where(lane < EDGE // 2, y, x)
+
+
 def beside(parts):
     c = lax.axis_index("col")
     return lax.rem(c + parts - 1, parts), lax.rem(c + 1, parts)
@@ -226,10 +239,12 @@
             for h in range(2):
                 row = PAD + HALF * h + 8 * g
                 ext[k, tiles - 1, row:row + 8, :] = unpack_edges(left, right, k, h)
-    for k in range(2):
-        for c in range(piece_ref.shape[0]):
-            for j in range(tiles):
-                ext[5 + k, j, PAD + 8 * c:PAD + 8 * c + 8, :] = piece_ref[c, tiles * k + j]
+    for c in range(piece_ref.shape[0]):
+        halos = split_halos(piece_ref[c, DTILES - 1])
+        for k in range(2):
+            for j in range(tiles - 1):
+                ext[5 + k, j, PAD + 8 * c:PAD + 8 * c + 8, :] = piece_ref[c, (tiles - 1) * k + j]
+            ext[5 + k, tiles - 1, PAD + 8 * c:PAD + 8 * c + 8, :] = halos[k]
     for k in range(7):
         place(k, 0, top_ref[k])
         place(k, PAD + rows, bot_ref[k])
@@ -243,7 +258,7 @@
     wrap_prim(prim)
     sub = lax.broadcasted_iota(jnp.int32, (8, cols + EDGE), 0)
     for ref, at, hit in ((top_ref, 1, 0), (bot_ref, BAND + 2, 7)):
-        outer = [jnp.broadcast_to(ref[7, k:k + 1], (8, cols + EDGE)) for k in range(4)]
+        outer = [jnp.broadcast_to(ref[4, k:k + 1], (8, cols + EDGE)) for k in range(4)]
         extra = primitives_of(*outer, outer[0])
         for k in (0, 3):
             prim[k, at] = jnp.where(sub == hit, extra[k], prim[k, at])
@@ -334,7 +349,7 @@
 def pack(first_ref, last_ref, disp_ref, piece_ref):
     parts = piece_ref.shape[0]
     tiles = DTILES // 2
-    cols = EDGE * (tiles - 1)
+    cols = EDGE * tiles
     before, after = beside(parts)
     lane = lax.broadcasted_iota(jnp.int32, (8, EDGE), 1)
     for g in range(HALF // 8):
@@ -353,12 +368,13 @@
         right = cols * ((c + 1) % parts)
         left = cols * ((c - 1) % parts) + cols - EDGE
         for k in range(2):
-            for j in range(tiles - 1):
+            for j in range(tiles):
                 at = cols * c + EDGE * j
                 piece_ref[c, tiles * k + j] = disp_ref[k, :, at:at + EDGE]
-            piece_ref[c, tiles * k + tiles - 1] = jnp.where(
-                lane < EDGE // 2, disp_ref[k, :, right:right + EDGE], disp_ref[k, :, left:left + EDGE]
-            )
+        piece_ref[c, DTILES - 1] = join_halos(
+            [disp_ref[k, :, right:right + EDGE] for k in range(2)],
+            [disp_ref[k, :, left:left + EDGE] for k in range(2)],
+        )
 
 
 def rim(top_ref, bot_ref, piece_ref, up_ref, down_ref):
@@ -370,22 +386,39 @@
     final = DTILES + HALF // 8 - 1
     l0, r0 = piece_ref[before, DTILES], piece_ref[after, DTILES]
     l1, r1 = piece_ref[before, final], piece_ref[after, final]
-    for k in range(5):
+    l2, r2 = piece_ref[before, DTILES + 1], piece_ref[after, DTILES + 1]
+    l3, r3 = piece_ref[before, final - 1], piece_ref[after, final - 1]
+
+    def inner(k):
         up_ref[k, :, :cols] = top_ref[k, :8]
         up_ref[k, :, cols:] = unpack_edges(l0, r0, k, 0)
         down_ref[k, :, :cols] = bot_ref[k, end:]
         down_ref[k, :, cols:] = unpack_edges(l1, r1, k, 1)
-    l0, r0 = piece_ref[before, DTILES + 1], piece_ref[after, DTILES + 1]
-    l1, r1 = piece_ref[before, final - 1], piece_ref[after, final - 1]
+
     for k in range(4):
-        up_ref[7, k:k + 1, :cols] = top_ref[k, 8:9]
-        up_ref[7, k:k + 1, cols:] = unpack_edges(l0, r0, k, 0)[:1]
-        down_ref[7, k:k + 1, :cols] = bot_ref[k, end - 1:end]
-        down_ref[7, k:k + 1, cols:] = unpack_edges(l1, r1, k, 1)[7:]
-    for k in range(2):
-        for j in range(tiles):
-            up_ref[5 + k, :, EDGE * j:EDGE * (j + 1)] = piece_ref[0, tiles * k + j]
-            down_ref[5 + k, :, EDGE * j:EDGE * (j + 1)] = piece_ref[parts - 1, tiles * k + j]
+        inner(k)
+    group = lax.axis_index("grp")
+
+    @pl.when(group == 0)
+    def _():
+        inner(4)
+
+    @pl.when(group == 1)
+    def _():
+        for k in range(4):
+            up_ref[4, k:k + 1, :cols] = top_ref[k, 8:9]
+            up_ref[4, k:k + 1, cols:] = unpack_edges(l2, r2, k, 0)[:1]
+            up_ref[4, 4 + k:5 + k, :] = jnp.zeros((1, cols + EDGE), jnp.float32)
+            down_ref[4, k:k + 1, :cols] = bot_ref[k, end - 1:end]
+            down_ref[4, k:k + 1, cols:] = unpack_edges(l3, r3, k, 1)[7:]
+            down_ref[4, 4 + k:5 + k, :] = jnp.zeros((1, cols + EDGE), jnp.float32)
+
+    for ref, c in ((up_ref, 0), (down_ref, parts - 1)):
+        halos = split_halos(piece_ref[c, DTILES - 1])
+        for k in range(2):
+            for j in range(tiles - 1):
+                ref[5 + k, :, EDGE * j:EDGE * (j + 1)] = piece_ref[c, (tiles - 1) * k + j]
+            ref[5 + k, :, cols:] = halos[k]
 
 
 def shift(x, axis, step):
@@ -412,7 +445,7 @@
         name="pack",
     )(conserved, conserved, displacement)
     pieces = lax.all_to_all(pieces, "col", 0, 0, tiled=True)
-    payload = pltpu.VMEM((8, 8, cols + EDGE), f32)
+    payload = pltpu.VMEM((7, 8, cols + EDGE), f32)
     up, down = pl.pallas_call(
         rim,
         out_shape=(payload, payload),

time: 45.2 us -> 44.6 us (0.987)
  no operation moved by 1% of the time
where the time goes in v4:
time: 44.6 us; the launch traced here: 44.3 us
  Pallas kernels  18.8 us (42%)
  blocking collectives  18.3 us (41%)
  starting transfers between devices  4.15 us (9%)
  waiting for transfers between devices  3.08 us (7%)
    all_to_all x1, blocking collectives, on_device(): pieces = lax.all_to_all(pieces, 'col', 0, 0, tiled=True)  18.3 us
    pallas_call x1, Pallas kernels, compute(): pl.pallas_call(core, out_shape=jax.ShapeDtypeStruct((1, 5, rows, cols), j...  16.3 us
    ppermute x2, starting transfers between devices, shift(): lax.ppermute(x, axis, [(i, (i + step) % count) for i in range(count)])  4.15 us
    ppermute x2, waiting for transfers between devices, shift(): lax.ppermute(x, axis, [(i, (i + step) % count) for i in range(count)])  3.08 us
    pallas_call x1, Pallas kernels, on_device(): pl.pallas_call(pack, out_shape=pltpu.VMEM((parts, DTILES + HALF // 8, 8,...  1.29 us
    pallas_call x1, Pallas kernels, on_device(): pl.pallas_call(rim, out_shape=(payload, payload), grid=(1,), in_specs=[at...  1.16 us
  transfers between devices with their start and end apart: 2, of which 1 were waited for; matrix products, arithmetic and copies ran while one was open for 0% of the time, Pallas kernels for 0%

profile of v4, /device:TPU:0, one launch (start us, length us, event | category | flops | bytes accessed | tf_op | source)
XLA Modules:
  0.0 44.3 jit_solution(17833480404754197992)
XLA Ops:
  0.0 1.3 %pack.1 = f32[8,13,8,128]{3,2,1,0:T(8,128)S(1)} custom-call(f32[5,64,512]{2,1,0:T(8,128)} %u_ref.1, f32[5,64,512]{2,1,0:T(8,128)} %u_ref.1, f32[2,8,4096]{2,1,0:T(8,128)} %disp_ref.1), custom_call_target="tpu_custom_call" | custom-call | tf_op jit(solution)/shard_map/pack/pallas_call | solution.py:435
  1.3 18.3 %all_to_all.5.piece_ref = f32[8,13,8,128]{3,2,1,0:T(8,128)S(1)} all-to-all(f32[8,13,8,128]{3,2,1,0:T(8,128)S(1)} %pack.1), channel_id=1, replica_groups=mesh['grp'=2,'row'=8,'col'=8] {'col'}, dimensions={0} | all-to-all | bytes 851968 | tf_op jit(solution)/shard_map/all_to_all | solution.py:447
  19.6 1.2 %rim.1 = (f32[7,8,640]{2,1,0:T(8,128)S(1)}, f32[7,8,640]{2,1,0:T(8,128)S(1)}) custom-call(f32[5,64,512]{2,1,0:T(8,128)} %u_ref.1, f32[5,64,512]{2,1,0:T(8,128)} %u_ref.1, f32[8,13,8,128]{3,2,1,0:T(8,128)S(1)} %all_to_all.5.piece_ref), custom_call_target="tpu_custom_call" | custom-call | tf_op jit(solution)/shard_map/rim/pallas_call | solution.py:449
  20.7 1.6 %collective-permute-start = (f32[7,8,640]{2,1,0:T(8,128)S(1)}, f32[7,8,640]{2,1,0:T(8,128)S(1)}, u32[]{:S(2)}, u32[]{:S(2)}) collective-permute-start(f32[7,8,640]{2,1,0:T(8,128)S(1)} %get-tuple-element.7), channel_id=1, source_target_pairs={{0,8},{8,16},{16,24},{24,32},{32,40},{40,48},{48,56},{56,0},{1,9},... | collective-permute-start | bytes 430088 | tf_op jit(solution)/shard_map/ppermute | solution.py:426
  22.3 2.6 %collective-permute-start.1 = (f32[7,8,640]{2,1,0:T(8,128)S(1)}, f32[7,8,640]{2,1,0:T(8,128)S(1)}, u32[]{:S(2)}, u32[]{:S(2)}) collective-permute-start(f32[7,8,640]{2,1,0:T(8,128)S(1)} %get-tuple-element.8), channel_id=1, source_target_pairs={{0,56},{8,0},{16,8},{24,16},{32,24},{40,32},{48,40},{56,48},{1,57}... | collective-permute-start | bytes 430088 | tf_op jit(solution)/shard_map/ppermute | solution.py:426
  24.9 3.1 %collective-permute-done.top_ref = f32[7,8,640]{2,1,0:T(8,128)S(1)} collective-permute-done((f32[7,8,640]{2,1,0:T(8,128)S(1)}, f32[7,8,640]{2,1,0:T(8,128)S(1)}, u32[]{:S(2)}, u32[]{:S(2)}) %collective-permute-start) | collective-permute-done | bytes 143392 | tf_op jit(solution)/shard_map/ppermute | solution.py:426
  27.9 0.0 collective-permute-done.1.bot_ref
  27.9 16.3 %euler_mesh.1 = f32[1,5,64,512]{3,2,1,0:T(8,128)} custom-call(f32[5,64,512]{2,1,0:T(8,128)} %u_ref.1, f32[8,13,8,128]{3,2,1,0:T(8,128)S(1)} %all_to_all.5.piece_ref, f32[7,8,640]{2,1,0:T(8,128)S(1)} %collective-permute-done.top_ref, f32[7,8,640]{2,1,0:T(8,128)S(1)} %collective-permute-done.1.bot_ref), custom_call_target="tpu_custom_call" | custom-call | tf_op jit(solution)/shard_map/euler_mesh/pallas_call | solution.py:333
Async XLA Ops:
  20.7 7.2 %collective-permute-start = (f32[7,8,640]{2,1,0:T(8,128)S(1)}, f32[7,8,640]{2,1,0:T(8,128)S(1)}, u32[]{:S(2)}, u32[]{:S(2)}) collective-permute-start(f32[7,8,640]{2,1,0:T(8,128)S(1)} %get-tuple-element.7), channel_id=1, source_target_pairs={{0,8},{8,16},{16,24},{24,32},{32,40},{40,48},{48,56},{56,0},{1,9},... | collective-permute-start | bytes 430088 | tf_op jit(solution)/shard_map/ppermute | solution.py:426
  22.3 5.6 %collective-permute-start.1 = (f32[7,8,640]{2,1,0:T(8,128)S(1)}, f32[7,8,640]{2,1,0:T(8,128)S(1)}, u32[]{:S(2)}, u32[]{:S(2)}) collective-permute-start(f32[7,8,640]{2,1,0:T(8,128)S(1)} %get-tuple-element.8), channel_id=1, source_target_pairs={{0,56},{8,0},{16,8},{24,16},{32,24},{40,32},{48,40},{56,48},{1,57}... | collective-permute-start | bytes 430088 | tf_op jit(solution)/shard_map/ppermute | solution.py:426
